TPU v7x, 256 devices: a whole 4x4x8 slice. The times are simulated.
256 devices in a mesh: stream: 16 (over z, core), cross: 16 (over x, y).
Axes of the slice: x: 4, y: 4, z: 8, core: 2. Of those that a mesh axis runs over, the one named last changes fastest.
Arguments:
- forcing: float32 [16, 16, 8, 128, 128], P('stream', 'cross'), may hold values from -6 to 6
- block_fine: float32 [16, 16, 8, 128, 128], P('stream', 'cross'), may hold values from -1 to 2
- couple_fine: float32 [16, 16, 8, 128, 128], P('stream', 'cross'), may hold values from -1 to 1
- pattern_fine: int32 [16, 16, 8], P('stream', 'cross'), may hold values from 0 to 7
- restrict_fine: int32 [16, 16, 256], P('stream', 'cross'), may hold values from 0 to 159
- landing_one: int32 [16, 16, 32], P('stream', 'cross'), may hold values from 0 to 127
- block_mid: float32 [16, 16, 4, 128, 128], P('stream', 'cross'), may hold values from -1 to 2
- couple_mid: float32 [16, 16, 4, 128, 128], P('stream', 'cross'), may hold values from -1 to 1
- pattern_mid: int32 [16, 16, 4], P('stream', 'cross'), may hold values from 0 to 3
- restrict_mid: int32 [16, 16, 128], P('stream', 'cross'), may hold values from 0 to 79
- landing_two: int32 [16, 16, 16], P('stream', 'cross'), may hold values from 0 to 63
- block_low: float32 [16, 16, 2, 128, 128], P('stream', 'cross'), may hold values from -1 to 2
- owner_cells: int32 [16, 16, 64], P('stream', 'cross'), may hold values from 0 to 127
- coarse_inverse: float32 [16, 512, 512], P('stream', 'cross'), may hold values from -1 to 2
Outputs:
- smooth_fine: float32 [16, 16, 8, 128, 128], P('stream', 'cross')
- smooth_mid: float32 [16, 16, 4, 128, 128], P('stream', 'cross')
- smooth_low: float32 [16, 16, 2, 128, 128], P('stream', 'cross')
- coarse_fix: float32 [16, 512, 128], P('stream', 'cross')
All inputs are finite; a program needn't handle non-finite values.
Results may differ from a plain program's by a relative error of at most 0.0003.
Values sent between devices are 32-bit elements; how exact they have to be, the bound alone decides.
A program may use at most 64 MiB of HBM per device.

v0:
```python
import jax
import jax.numpy as jnp
from jax import lax
from jax.sharding import PartitionSpec as P

BCELL = 32
CHEB = 6
M1 = 128
S1 = 32
M2 = 64
S2 = 16


centre = 1.0
spread = 0.5
coarse_weight = 0.5


def from_behind(value, axis, steps):
    count = lax.axis_size(axis)
    pairs = [(source, (source + steps) % count) for source in range(count)]
    return lax.ppermute(value, axis, pairs)


def apply_blocks(diagonal_blocks, coupling, pattern, vector):
    result = jnp.einsum("bij,bjr->bir", diagonal_blocks, vector, precision=lax.Precision.HIGHEST)
    if coupling is not None:
        result = result + jnp.einsum(
            "bij,bjr->bir",
            coupling,
            jnp.take(vector, pattern, axis=0),
            precision=lax.Precision.HIGHEST,
        )
    return result


def chebyshev(diagonal_blocks, coupling, pattern, source):
    ratio_bound = centre / spread
    momentum = 1.0 / ratio_bound
    update = source / centre
    answer = update
    residual = source
    for sweep_index in range(CHEB):
        residual = residual - apply_blocks(diagonal_blocks, coupling, pattern, update)
        momentum_next = 1.0 / (2.0 * ratio_bound - momentum)
        update = momentum_next * momentum * update + 2.0 * momentum_next / spread * residual
        answer = answer + update
        momentum = momentum_next
    residual = residual - apply_blocks(diagonal_blocks, coupling, pattern, update)
    return (answer, residual)


def cell_rows(vector, cell_count):
    block_count, unknowns, columns = vector.shape
    return (
        vector.reshape(block_count, 4, cell_count, columns)
        .transpose(0, 2, 1, 3)
        .reshape(block_count * cell_count, 4 * columns)
    )


def block_rows(rows, cell_count):
    total_rows, width_all = rows.shape
    columns = width_all // 4
    block_count = total_rows // cell_count
    return (
        rows.reshape(block_count, cell_count, 4, columns)
        .transpose(0, 2, 1, 3)
        .reshape(block_count, 4 * cell_count, columns)
    )


def summed_by(cell_map, rows, segments):
    targets = lax.broadcasted_iota(jnp.int32, (segments, cell_map.shape[0]), 0)
    selector = (targets == cell_map[None, :]).astype(jnp.float32)
    return jnp.dot(selector, rows, precision=lax.Precision.HIGHEST)


def restrict(residual, cell_map, segments):
    return coarse_weight * summed_by(cell_map, cell_rows(residual, BCELL), segments)


def add_landed(owned_rows, arrived, landing):
    return owned_rows + summed_by(landing, arrived, owned_rows.shape[0])


def on_device(
    forcing,
    block_fine,
    couple_fine,
    pattern_fine,
    restrict_fine,
    landing_one,
    block_mid,
    couple_mid,
    pattern_mid,
    restrict_mid,
    landing_two,
    block_low,
    owner_cells,
    coarse_inverse,
):
    inverse_rows = coarse_inverse[0]
    answer_fine, residual_fine = chebyshev(
        block_fine[0, 0], couple_fine[0, 0], pattern_fine[0, 0], forcing[0, 0]
    )
    partial_value = restrict(residual_fine, restrict_fine[0, 0], M1 + S1)
    arrived = from_behind(partial_value[M1:], "stream", 1)
    source_mid = block_rows(add_landed(partial_value[:M1], arrived, landing_one[0, 0]), BCELL)
    answer_mid, residual_mid = chebyshev(
        block_mid[0, 0], couple_mid[0, 0], pattern_mid[0, 0], source_mid
    )
    partial_two = restrict(residual_mid, restrict_mid[0, 0], M2 + S2)
    arrived_two = from_behind(partial_two[M2:], "stream", 1)
    source_low = block_rows(add_landed(partial_two[:M2], arrived_two, landing_two[0, 0]), BCELL)
    answer_low, residual_low = chebyshev(block_low[0, 0], None, None, source_low)
    group_cells = coarse_inverse.shape[2] // 4
    partial_three = restrict(residual_low, owner_cells[0, 0], group_cells)
    flat_three = partial_three.reshape(group_cells * 4, partial_three.shape[1] // 4)
    owned_share = lax.psum_scatter(flat_three, "cross", scatter_dimension=0, tiled=True)
    correction = jnp.dot(
        inverse_rows,
        lax.all_gather(owned_share, "cross", axis=0, tiled=True),
        precision=lax.Precision.HIGHEST,
    )
    return (
        answer_fine[None, None],
        answer_mid[None, None],
        answer_low[None, None],
        correction[None],
    )


def solution(mesh):
    return jax.shard_map(
        on_device,
        mesh=mesh,
        in_specs=(
            P("stream", "cross", None, None, None),
            P("stream", "cross", None, None, None),
            P("stream", "cross", None, None, None),
            P("stream", "cross", None),
            P("stream", "cross", None),
            P("stream", "cross", None),
            P("stream", "cross", None, None, None),
            P("stream", "cross", None, None, None),
            P("stream", "cross", None),
            P("stream", "cross", None),
            P("stream", "cross", None),
            P("stream", "cross", None, None, None),
            P("stream", "cross", None),
            P("stream", "cross", None),
        ),
        out_specs=(
            P("stream", "cross", None, None, None),
            P("stream", "cross", None, None, None),
            P("stream", "cross", None, None, None),
            P("stream", "cross", None),
        ),
        check_vma=False,
    )
```

profile of v0, /device:TPU:2, one launch (start us, length us, event | category | flops | bytes accessed | tf_op | source)
XLA Modules:
  0.0 177.9 jit_solution(4751336302082331956)
XLA Ops:
  7.2 0.7 compare_select_fusion.1
  8.0 1.6 gather_fusion
  9.6 0.7 convolution_bitcast_fusion
  10.8 0.8 multiply_add_fusion.5
  11.6 1.4 gather_fusion.1
  13.0 0.6 fusion.53
  14.0 0.8 multiply_add_fusion.4
  14.8 1.4 gather_fusion.2
  16.2 0.6 fusion.51
  17.2 1.6 multiply_add_fusion.3
  18.8 1.4 gather_fusion.3
  20.2 0.6 fusion.49
  21.4 1.6 multiply_add_fusion.2
  22.9 1.4 gather_fusion.4
  24.3 0.6 fusion.47
  25.5 1.7 multiply_add_fusion.1
  27.2 2.4 %gather_fusion.5 = f32[8,128,128]{2,1,0:T(8,128)} fusion(f32[8,128,128]{2,1,0:T(8,128)} %get-tuple-element.18, s32[1024]{0:T(1024)S(1)} %pad_clamp_fusion.1), kind=kCustom, calls=%fused_computation.6.clone | custom fusion | bytes 1048608 | tf_op jit(solution)/shard_map/jit(_take)/gather | solution.py:31
  29.7 1.8 fusion.45
  31.5 0.7 fusion.3
  32.7 1.3 add_bitcast_fusion
  34.0 1.7 gather_fusion.6
  35.7 0.6 fusion.43
  36.7 0.7 fusion.1
  37.8 0.7 copy-done.21
  38.9 0.6 copy-done.27
  39.5 6.6 %collective-permute-done = f32[32,512]{1,0:T(8,128)S(1)} collective-permute-done((f32[32,512]{1,0:T(8,128)S(1)}, f32[32,512]{1,0:T(8,128)S(1)}, u32[]{:S(2)}, u32[]{:S(2)}) %collective-permute-start) | collective-permute-done | bytes 65568 | tf_op jit(solution)/shard_map/ppermute | solution.py:22
  46.5 0.6 gather_fusion.7
  47.8 0.6 copy-done.3
  48.4 0.7 multiply_add_fusion.11
  49.1 0.6 gather_fusion.8
  50.5 0.6 gather_fusion.9
  51.5 0.5 multiply_add_fusion.9
  52.0 0.6 gather_fusion.10
  53.0 1.2 multiply_add_fusion.8
  54.2 0.6 gather_fusion.11
  55.1 0.6 copy-done.19
  56.2 0.6 gather_fusion.12
  57.6 0.8 add_bitcast_fusion.1
  58.4 0.6 gather_fusion.13
  60.1 0.6 copy-done.22
  61.0 4.5 %collective-permute-done.1 = f32[16,512]{1,0:T(8,128)S(1)} collective-permute-done((f32[16,512]{1,0:T(8,128)S(1)}, f32[16,512]{1,0:T(8,128)S(1)}, u32[]{:S(2)}, u32[]{:S(2)}) %collective-permute-start.1) | collective-permute-done | bytes 32800 | tf_op jit(solution)/shard_map/ppermute | solution.py:22
  65.8 0.9 copy-done.5
  68.9 0.6 copy-done.24
  69.8 0.7 reshape.66
  70.5 0.7 add_bitcast_fusion.2
  71.3 76.8 %reduce-scatter.2.cloned.1.call-done = f32[32,128]{1,0:T(8,128)} async-done(((f32[512,128]{1,0:T(8,128)}), f32[32,128]{1,0:T(8,128)}) %reduce-scatter.2.cloned.1.call-update) | async-done | bytes 16400 | tf_op jit(solution)/shard_map/reduce_scatter | solution.py:120
  148.0 22.1 %all_gather.3 = f32[512,128]{1,0:T(8,128)S(1)} all-gather(f32[32,128]{1,0:T(8,128)} %reduce-scatter.2.cloned.1.call-done), channel_id=1, replica_groups=mesh['stream'=16,'cross'=16] {'cross'}, dimensions={0}, use_global_device_ids=true | all-gather | bytes 278528 | tf_op jit(solution)/shard_map/all_gather | solution.py:123
  170.2 0.9 convolution_bitcast_fusion.8
  (90 shorter events, 12.5 us)
Async XLA Ops:
  7.2 2.4 %copy-start = (f32[1,1,8,128,128]{4,3,2,1,0:T(8,128)S(1)}, f32[1,1,8,128,128]{4,3,2,1,0:T(8,128)}, u32[]{:S(2)}) copy-start(f32[1,1,8,128,128]{4,3,2,1,0:T(8,128)} %param.20) | copy-start | bytes 1572868
  7.2 0.8 copy-start.26
  7.2 140.9 %reduce-scatter.2.cloned.1.call-start = ((), (), s32[]{:S(2)}) async-start(), calls=%async_computation.1 | async-start | bytes 278528 | tf_op jit(solution)/shard_map/reduce_scatter | solution.py:120
  9.6 1.0 copy-start.1
  9.6 1.2 copy-start.6
  13.0 1.0 copy-start.14
  16.2 1.0 copy-start.15
  20.2 1.0 copy-start.11
  20.2 1.2 copy-start.16
  24.3 1.0 copy-start.12
  24.3 1.2 copy-start.17
  29.7 1.8 copy-start.13
  29.7 1.8 %copy-start.18 = (f32[8,128,128]{2,1,0:T(8,128)S(1)}, f32[8,128,128]{2,1,0:T(8,128)}, u32[]{:S(2)}) copy-start(f32[8,128,128]{2,1,0:T(8,128)} %gather_fusion.5) | copy-start | bytes 1572868
  31.5 1.0 copy-start.4
  31.5 1.2 copy-start.7
  32.7 1.3 copy-start.9
  34.0 1.7 copy-start.8
  35.7 1.0 copy-start.10
  37.8 0.7 copy-start.21
  38.8 0.7 copy-start.27
  38.9 7.3 %collective-permute-start = (f32[32,512]{1,0:T(8,128)S(1)}, f32[32,512]{1,0:T(8,128)S(1)}, u32[]{:S(2)}, u32[]{:S(2)}) collective-permute-start(f32[32,512]{1,0:T(8,128)S(1)} %slice.45), channel_id=1, source_target_pairs={{0,16},{16,32},{32,48},{48,64},{64,80},{80,96},{96,112},{112,128},... | collective-permute-start | bytes 196616 | tf_op jit(solution)/shard_map/ppermute | solution.py:22
  39.5 6.6 %copy-start.25 = (s32[1,1,32]{2,1,0:T(1,128)S(1)}, s32[1,1,32]{2,1,0:T(1,128)}, u32[]{:S(2)}) copy-start(s32[1,1,32]{2,1,0:T(1,128)} %param.23) | copy-start | bytes 388
  46.5 1.0 copy-start.2
  47.5 0.9 copy-start.3
  54.8 1.0 copy-start.19
  60.0 0.7 copy-start.22
  61.0 4.6 %copy-start.23 = (s32[1,1,16]{2,1,0:T(1,128)S(1)}, s32[1,1,16]{2,1,0:T(1,128)}, u32[]{:S(2)}) copy-start(s32[1,1,16]{2,1,0:T(1,128)} %param.28) | copy-start | bytes 196
  61.0 4.6 %collective-permute-start.1 = (f32[16,512]{1,0:T(8,128)S(1)}, f32[16,512]{1,0:T(8,128)S(1)}, u32[]{:S(2)}, u32[]{:S(2)}) collective-permute-start(f32[16,512]{1,0:T(8,128)S(1)} %slice.47), channel_id=1, source_target_pairs={{0,16},{16,32},{32,48},{48,64},{64,80},{80,96},{96,112},{112,128},... | collective-permute-start | bytes 98312 | tf_op jit(solution)/shard_map/ppermute | solution.py:22
  65.8 0.9 copy-start.5
  68.9 0.7 copy-start.24
  71.3 98.9 %copy-start.20 = (f32[1,32,512]{2,1,0:T(8,128)S(1)}, f32[1,32,512]{2,1,0:T(8,128)}, u32[]{:S(2)}) copy-start(f32[1,32,512]{2,1,0:T(8,128)} %param.31) | copy-start | bytes 196612
Sparse Core Ops, SparseCore 0:
  70.6 77.3 reduce-scatter.1
where the time goes:
time: 179 us; the launch traced here: 178 us
  waiting for transfers between devices  87.9 us (49%)
  local copies, waits for them, and re-layouts  25 us (14%)
  matrix products  24.6 us (14%)
  blocking collectives  22.1 us (12%)
  between operations  14.7 us (8%)
  other arithmetic  3.56 us (2%)
    reduce_scatter x1, waiting for transfers between devices, on_device(): lax.psum_scatter(flat_three, 'cross', scatter_dimension=0, tiled=True)  76.8 us
    all_gather x1, blocking collectives, on_device(): lax.all_gather(owned_share, 'cross', axis=0, tiled=True)  22.1 us
    gather x14, local copies, waits for them, and re-layouts, apply_blocks(): jnp.take(vector, pattern, axis=0)  15.2 us
    dot_general x14, matrix products, apply_blocks(): jnp.einsum('bij,bjr->bir', coupling, jnp.take(vector, pattern, axis=0), p...  12.1 us
    ppermute x2, waiting for transfers between devices, from_behind(): return lax.ppermute(value, axis, pairs)  11.1 us
    dot_general x21, matrix products, apply_blocks(): jnp.einsum('bij,bjr->bir', diagonal_blocks, vector, precision=lax.Precisi...  10.3 us
    unnamed x56, local copies, waits for them, and re-layouts  8.28 us
  transfers between devices with their start and end apart: 3, of which 3 were waited for; matrix products, arithmetic and copies ran while one was open for 0% of the time, Pallas kernels for 0%

commit v1 on v0

v1 whole, which is shorter than its diff:
```python
import functools

import jax
import jax.numpy as jnp
from jax import lax
from jax.experimental import pallas as pl
from jax.experimental.pallas import tpu as pltpu
from jax.sharding import PartitionSpec as P

MESH = pl.DeviceIdType.MESH
BCELL = 32
CHEB = 6
M1 = 128
S1 = 32
M2 = 64
S2 = 16
UNK = 128
R = 128
NB0 = 8
NB1 = 4
NB2 = 2
COARSE = 512

centre = 1.0
spread = 0.5
coarse_weight = 0.5

f32 = jnp.float32
bf16 = jnp.bfloat16


def coefficients():
    ratio_bound = centre / spread
    momentum = 1.0 / ratio_bound
    pairs = []
    for _ in range(CHEB):
        momentum_next = 1.0 / (2.0 * ratio_bound - momentum)
        pairs.append((momentum_next * momentum, 2.0 * momentum_next / spread))
        momentum = momentum_next
    return pairs


STEPS = coefficients()


def dot(a, b):
    return jnp.dot(a, b, preferred_element_type=f32)


def split(value):
    high = value.astype(bf16)
    return high, (value - high.astype(f32)).astype(bf16)


def halves(value):
    return jnp.concatenate(split(value), axis=1)


def product(matrix, vector):
    rows = matrix.shape[0] // 2
    both = dot(matrix[:rows], vector)
    return both[:, :R] + both[:, R:] + dot(matrix[rows:], vector[:, :R])


def stack_parts(target, b, column, value):
    high, low = split(value)
    target[b, :UNK, column : column + UNK] = high
    target[b, UNK:, column : column + UNK] = low


def smoothing(blocks, pattern, source, operator, vectors, answer, residual, update, answer_ready, finish):
    for step in range(CHEB + 1):
        now, later = vectors[step % 2], vectors[(step + 1) % 2]
        for b in range(blocks):
            own = now[b]
            if pattern is not None:
                own = jnp.concatenate([own, now[pattern[b]]], axis=0)
            left = (source[b] if step == 0 else residual[b]) - product(operator[b], own)
            if step == CHEB:
                finish(b, left)
                continue
            residual[b] = left
            keep, gain = STEPS[step]
            changed = keep * (source[b] if step == 0 else update[b]) + gain * left
            if step < CHEB - 1:
                update[b] = changed
            answer[b] = (source[b] if step == 0 else answer[b]) + changed
            later[b] = halves(changed)
        if step == CHEB - 1:
            answer_ready()


def selector(rows, targets, weight):
    wanted = lax.broadcasted_iota(jnp.int32, (rows, targets.shape[1]), 0)
    return jnp.where(wanted == targets, jnp.float32(weight), jnp.float32(0.0)).astype(bf16)


def gathered(matrix, vector):
    both = dot(matrix, vector)
    return both[:, :R] + both[:, R:]


def kernel(
    n_stream,
    n_cross,
    pattern_fine,
    pattern_mid,
    restrict_fine,
    landing_one,
    restrict_mid,
    landing_two,
    owner_cells,
    forcing,
    block_fine,
    couple_fine,
    block_mid,
    couple_mid,
    block_low,
    inverse,
    out_fine,
    out_mid,
    out_low,
    out_fix,
    f_fine,
    d_fine,
    c_fine,
    a_fine,
    v_fine0,
    v_fine1,
    x_fine,
    r_fine,
    u_fine,
    p_fine,
    d_mid,
    c_mid,
    a_mid,
    f_mid,
    v_mid0,
    v_mid1,
    x_mid,
    r_mid,
    u_mid,
    p_mid,
    d_low,
    a_low,
    e_low,
    v_low0,
    v_low1,
    x_low,
    r_low,
    u_low,
    pq_low,
    f_low,
    p_low,
    y_low,
    inv,
    inv_parts,
    send_one,
    got_one,
    send_two,
    got_two,
    partial,
    slots,
    share,
    coarse,
    fix,
    load_f,
    load_d,
    load_c,
    load_rest,
    store_sem,
    one_send,
    one_recv,
    two_send,
    two_recv,
    rs_send,
    rs_recv,
    ag_send,
    ag_recv,
):
    me_s = lax.axis_index("stream")
    me_c = lax.axis_index("cross")
    ahead = lax.rem(me_s + 1, n_stream)
    behind = lax.rem(me_s + n_stream - 1, n_stream)
    share_rows = COARSE // n_cross

    def start(source, target, sem):
        copy = pltpu.make_async_copy(source, target, sem)
        copy.start()
        return copy

    copy_f = start(forcing, f_fine, load_f)
    copies_d = []
    copies_c = []
    for b in range(NB0):
        copies_d.append(start(block_fine.at[b], d_fine.at[b], load_d.at[b]))
        copies_c.append(start(couple_fine.at[b], c_fine.at[b], load_c.at[b]))
    copy_dm = start(block_mid, d_mid, load_rest.at[0])
    copy_cm = start(couple_mid, c_mid, load_rest.at[1])
    copy_dl = start(block_low, d_low, load_rest.at[2])
    copy_inv = start(inverse, inv, load_rest.at[3])

    barrier = pltpu.get_barrier_semaphore()
    for peer in (ahead, behind):
        pl.semaphore_signal(barrier, inc=1, device_id={"stream": peer}, device_id_type=MESH)
    for offset in range(1, n_cross):
        peer = lax.rem(me_c + offset, n_cross)
        pl.semaphore_signal(barrier, inc=1, device_id={"cross": peer}, device_id_type=MESH)

    copy_f.wait()
    for b in range(NB0):
        v_fine0[b] = halves(f_fine[b])
    for b in range(NB0):
        copies_d[b].wait()
        stack_parts(a_fine, b, 0, d_fine[b])
        copies_c[b].wait()
        stack_parts(a_fine, b, UNK, c_fine[b])

    stores = []

    def finish_fine(b, value):
        p_fine[b] = halves(value)

    smoothing(
        NB0,
        pattern_fine,
        f_fine,
        a_fine,
        (v_fine0, v_fine1),
        x_fine,
        r_fine,
        u_fine,
        lambda: stores.append(start(x_fine, out_fine, store_sem.at[0])),
        finish_fine,
    )

    pl.semaphore_wait(barrier, n_cross + 1)

    def to_next(c, source, target, send_sems, recv_sems):
        return pltpu.make_async_remote_copy(
            src_ref=source.at[c],
            dst_ref=target.at[c],
            send_sem=send_sems.at[c],
            recv_sem=recv_sems.at[c],
            device_id={"stream": ahead},
            device_id_type=MESH,
        )

    pick = selector(M1 + S1, restrict_fine[...], coarse_weight)
    to_one = []
    for c in range(4):
        rows = p_fine[:, c * BCELL : (c + 1) * BCELL, :].reshape(NB0 * BCELL, 2 * R)
        sums = gathered(pick, rows)
        send_one[c] = sums[M1:]
        copy = to_next(c, send_one, got_one, one_send, one_recv)
        copy.start()
        to_one.append(copy)
        for b in range(NB1):
            f_mid[b, c * BCELL : (c + 1) * BCELL, :] = sums[b * BCELL : (b + 1) * BCELL]

    copy_dm.wait()
    copy_cm.wait()
    for b in range(NB1):
        stack_parts(a_mid, b, 0, d_mid[b])
        stack_parts(a_mid, b, UNK, c_mid[b])
    copy_dl.wait()
    row = lax.broadcasted_iota(jnp.int32, (UNK, UNK), 0)
    column = lax.broadcasted_iota(jnp.int32, (UNK, UNK), 1)
    for b in range(NB2):
        stack_parts(a_low, b, 0, d_low[b])
        e_low[b] = jnp.where(row == column, jnp.float32(1.0), jnp.float32(0.0))
        v_low0[b] = halves(e_low[b])

    def finish_low(b, value):
        high, low = split(x_low[b])
        pq_low[b, 0:UNK] = high
        pq_low[b, UNK : 2 * UNK] = low
        high, low = split(value)
        pq_low[b, 2 * UNK : 3 * UNK] = high
        pq_low[b, 3 * UNK :] = low

    smoothing(
        NB2,
        None,
        e_low,
        a_low,
        (v_low0, v_low1),
        x_low,
        r_low,
        u_low,
        lambda: None,
        finish_low,
    )
    land = selector(M1, landing_one[...], 1.0)

    for c in range(4):
        to_one[c].wait_recv()
        landed = gathered(land, halves(got_one[c]))
        for b in range(NB1):
            cells = slice(c * BCELL, (c + 1) * BCELL)
            source = f_mid[b, cells, :] + landed[b * BCELL : (b + 1) * BCELL]
            f_mid[b, cells, :] = source
            v_mid0[b, cells, :] = halves(source)

    def finish_mid(b, value):
        p_mid[b] = halves(value)

    smoothing(
        NB1,
        pattern_mid,
        f_mid,
        a_mid,
        (v_mid0, v_mid1),
        x_mid,
        r_mid,
        u_mid,
        lambda: stores.append(start(x_mid, out_mid, store_sem.at[1])),
        finish_mid,
    )

    pick = selector(M2 + S2, restrict_mid[...], coarse_weight)
    to_two = []
    for c in range(4):
        rows = p_mid[:, c * BCELL : (c + 1) * BCELL, :].reshape(NB1 * BCELL, 2 * R)
        sums = gathered(pick, rows)
        send_two[c] = sums[M2:]
        copy = to_next(c, send_two, got_two, two_send, two_recv)
        copy.start()
        to_two.append(copy)
        for b in range(NB2):
            f_low[b, c * BCELL : (c + 1) * BCELL, :] = sums[b * BCELL : (b + 1) * BCELL]

    copy_inv.wait()
    high, low = split(inv[...])
    inv_parts[:share_rows] = high
    inv_parts[share_rows:] = low
    owners = owner_cells[...] * 4
    targets = jnp.concatenate(
        [owners[:, b * BCELL : (b + 1) * BCELL] + c for b in range(NB2) for c in range(4)],
        axis=1,
    )
    land = selector(M2, landing_two[...], 1.0)

    for c in range(4):
        to_two[c].wait_recv()
        landed = gathered(land, halves(got_two[c]))
        for b in range(NB2):
            cells = slice(c * BCELL, (c + 1) * BCELL)
            f_low[b, cells, :] = f_low[b, cells, :] + landed[b * BCELL : (b + 1) * BCELL]

    for b in range(NB2):
        vector = halves(f_low[b])
        y_low[b] = product(pq_low[b, : 2 * UNK], vector)
        p_low[b] = halves(product(pq_low[b, 2 * UNK :], vector))
    stores.append(start(y_low, out_low, store_sem.at[2]))

    pick = selector(COARSE, targets, coarse_weight)
    rows = p_low[...].reshape(NB2 * UNK, 2 * R)
    partial[...] = gathered(pick, rows).reshape(n_cross, share_rows, R)

    scattered = []
    for offset in range(1, n_cross):
        peer = lax.rem(me_c + offset, n_cross)
        copy = pltpu.make_async_remote_copy(
            src_ref=partial.at[peer],
            dst_ref=slots.at[offset],
            send_sem=rs_send.at[offset],
            recv_sem=rs_recv.at[offset],
            device_id={"cross": peer},
            device_id_type=MESH,
        )
        copy.start()
        scattered.append(copy)
    total = partial[me_c]
    for offset in range(1, n_cross):
        scattered[offset - 1].wait_recv()
        total = total + slots[offset]
    share[...] = total

    spread_out = []
    for offset in range(1, n_cross):
        peer = lax.rem(me_c + offset, n_cross)
        copy = pltpu.make_async_remote_copy(
            src_ref=share,
            dst_ref=coarse.at[me_c],
            send_sem=ag_send.at[offset],
            recv_sem=ag_recv.at[offset],
            device_id={"cross": peer},
            device_id_type=MESH,
        )
        copy.start()
        spread_out.append(copy)
    coarse[me_c] = total
    for offset in range(1, n_cross):
        origin = lax.rem(me_c + n_cross - offset, n_cross)
        pltpu.make_async_remote_copy(
            src_ref=share,
            dst_ref=coarse.at[origin],
            send_sem=ag_send.at[offset],
            recv_sem=ag_recv.at[offset],
            device_id={"cross": lax.rem(me_c + offset, n_cross)},
            device_id_type=MESH,
        ).wait_recv()

    fix[...] = product(inv_parts[...], halves(coarse[...].reshape(COARSE, R)))
    stores.append(start(fix, out_fix, store_sem.at[3]))
    for copy in to_one + to_two + scattered + spread_out:
        copy.wait_send()
    for copy in stores:
        copy.wait()


def on_device(n_stream, n_cross, forcing, block_fine, couple_fine, pattern_fine, restrict_fine, landing_one,
              block_mid, couple_mid, pattern_mid, restrict_mid, landing_two, block_low, owner_cells, coarse_inverse):
    share_rows = COARSE // n_cross
    smem = pl.BlockSpec(memory_space=pltpu.SMEM)
    vmem = pl.BlockSpec(memory_space=pltpu.VMEM)
    anywhere = pl.BlockSpec(memory_space=pl.ANY)

    def vector(blocks):
        return pltpu.VMEM((blocks, UNK, R), f32)

    def parts(blocks):
        return pltpu.VMEM((blocks, UNK, 2 * R), bf16)

    def dma(*shape):
        return pltpu.SemaphoreType.DMA(shape)

    fine, mid, low, fix = pl.pallas_call(
        functools.partial(kernel, n_stream, n_cross),
        out_shape=(
            jax.ShapeDtypeStruct((NB0, UNK, R), f32),
            jax.ShapeDtypeStruct((NB1, UNK, R), f32),
            jax.ShapeDtypeStruct((NB2, UNK, R), f32),
            jax.ShapeDtypeStruct((share_rows, R), f32),
        ),
        in_specs=[smem] * 2 + [vmem] * 5 + [anywhere] * 7,
        out_specs=(anywhere,) * 4,
        scratch_shapes=[
            vector(NB0),
            vector(NB0),
            vector(NB0),
            pltpu.VMEM((NB0, 2 * UNK, 2 * UNK), bf16),
            parts(NB0),
            parts(NB0),
            vector(NB0),
            vector(NB0),
            vector(NB0),
            parts(NB0),
            vector(NB1),
            vector(NB1),
            pltpu.VMEM((NB1, 2 * UNK, 2 * UNK), bf16),
            vector(NB1),
            parts(NB1),
            parts(NB1),
            vector(NB1),
            vector(NB1),
            vector(NB1),
            parts(NB1),
            vector(NB2),
            pltpu.VMEM((NB2, 2 * UNK, UNK), bf16),
            vector(NB2),
            parts(NB2),
            parts(NB2),
            vector(NB2),
            vector(NB2),
            vector(NB2),
            pltpu.VMEM((NB2, 4 * UNK, UNK), bf16),
            vector(NB2),
            parts(NB2),
            vector(NB2),
            pltpu.VMEM((share_rows, COARSE), f32),
            pltpu.VMEM((2 * share_rows, COARSE), bf16),
            pltpu.VMEM((4, S1, R), f32),
            pltpu.VMEM((4, S1, R), f32),
            pltpu.VMEM((4, S2, R), f32),
            pltpu.VMEM((4, S2, R), f32),
            pltpu.VMEM((n_cross, share_rows, R), f32),
            pltpu.VMEM((n_cross, share_rows, R), f32),
            pltpu.VMEM((share_rows, R), f32),
            pltpu.VMEM((n_cross, share_rows, R), f32),
            pltpu.VMEM((share_rows, R), f32),
            pltpu.SemaphoreType.DMA,
            dma(NB0),
            dma(NB0),
            dma(4),
            dma(4),
            dma(4),
            dma(4),
            dma(4),
            dma(4),
            dma(n_cross),
            dma(n_cross),
            dma(n_cross),
            dma(n_cross),
        ],
        compiler_params=pltpu.CompilerParams(
            collective_id=0, has_side_effects=True, vmem_limit_bytes=48 << 20
        ),
        name="vcycle",
    )(
        pattern_fine.reshape(NB0),
        pattern_mid.reshape(NB1),
        restrict_fine.reshape(1, -1),
        landing_one.reshape(1, -1),
        restrict_mid.reshape(1, -1),
        landing_two.reshape(1, -1),
        owner_cells.reshape(1, -1),
        forcing[0, 0],
        block_fine[0, 0],
        couple_fine[0, 0],
        block_mid[0, 0],
        couple_mid[0, 0],
        block_low[0, 0],
        coarse_inverse[0],
    )
    return fine[None, None], mid[None, None], low[None, None], fix[None]


def solution(mesh):
    tile = P("stream", "cross", None, None, None)
    table = P("stream", "cross", None)
    return jax.shard_map(
        functools.partial(on_device, mesh.shape["stream"], mesh.shape["cross"]),
        mesh=mesh,
        in_specs=(tile, tile, tile, table, table, table, tile, tile, table, table, table, tile, table, table),
        out_specs=(tile, tile, tile, table),
        check_vma=False,
    )
```

time: 179 us -> 44 us (0.25)
  the two profiles are of different devices: /device:TPU:2 before, /device:TPU:8 now
where the time goes in v1:
time: 44 us; the launch traced here: 43.6 us
  Pallas kernels  32.7 us (74%)
  local copies, waits for them, and re-layouts  10.2 us (23%)
  between operations  0.71 us (2%)
    pallas_call x1, Pallas kernels, on_device(): pl.pallas_call(functools.partial(kernel, n_stream, n_cross), out_shape=(j...  32.7 us
    unnamed x32, local copies, waits for them, and re-layouts  10.2 us

profile of v1, /device:TPU:8, one launch (start us, length us, event | category | flops | bytes accessed | tf_op | source)
XLA Modules:
  0.0 43.6 jit_solution(9761755845827433954)
XLA Ops:
  0.6 0.0 copy-start.13
  0.6 0.0 copy-start.9
  0.7 0.0 copy-start.10
  0.7 0.0 copy-start.11
  0.7 0.0 copy-start.12
  0.7 0.0 copy-start.7
  0.7 0.0 copy-start.8
  0.7 0.6 %copy-done.13 = s32[1,1,64]{2,1,0:T(1,128)S(1)} copy-done((s32[1,1,64]{2,1,0:T(1,128)S(1)}, s32[1,1,64]{2,1,0:T(1,128)}, u32[]{:S(2)}) %copy-start.13) | copy-done | bytes 280
  1.3 0.0 copy-done.9
  1.3 0.0 copy-done.10
  1.3 0.0 copy-done.11
  1.3 0.0 copy-done.12
  1.4 0.0 copy-done.7
  1.4 0.0 copy-done.8
  1.4 0.0 copy-start
  1.4 1.0 %copy-done = f32[1,1,8,128,128]{4,3,2,1,0:T(8,128)S(1)} copy-done((f32[1,1,8,128,128]{4,3,2,1,0:T(8,128)S(1)}, f32[1,1,8,128,128]{4,3,2,1,0:T(8,128)}, u32[]{:S(2)}) %copy-start) | copy-done | bytes 524312
  2.4 0.0 copy-start.1
  2.4 1.0 %copy-done.1 = f32[1,1,8,128,128]{4,3,2,1,0:T(8,128)S(1)} copy-done((f32[1,1,8,128,128]{4,3,2,1,0:T(8,128)S(1)}, f32[1,1,8,128,128]{4,3,2,1,0:T(8,128)}, u32[]{:S(2)}) %copy-start.1) | copy-done | bytes 524312
  3.5 0.0 copy-start.2
  3.5 1.0 %copy-done.2 = f32[1,1,8,128,128]{4,3,2,1,0:T(8,128)S(1)} copy-done((f32[1,1,8,128,128]{4,3,2,1,0:T(8,128)S(1)}, f32[1,1,8,128,128]{4,3,2,1,0:T(8,128)}, u32[]{:S(2)}) %copy-start.2) | copy-done | bytes 524312
  4.5 0.0 copy-start.3
  4.5 0.9 %copy-done.3 = f32[1,1,4,128,128]{4,3,2,1,0:T(8,128)S(1)} copy-done((f32[1,1,4,128,128]{4,3,2,1,0:T(8,128)S(1)}, f32[1,1,4,128,128]{4,3,2,1,0:T(8,128)}, u32[]{:S(2)}) %copy-start.3) | copy-done | bytes 262168
  5.5 0.0 copy-start.4
  5.5 0.9 %copy-done.4 = f32[1,1,4,128,128]{4,3,2,1,0:T(8,128)S(1)} copy-done((f32[1,1,4,128,128]{4,3,2,1,0:T(8,128)S(1)}, f32[1,1,4,128,128]{4,3,2,1,0:T(8,128)}, u32[]{:S(2)}) %copy-start.4) | copy-done | bytes 262168
  6.4 0.0 copy-start.5
  6.4 0.9 %copy-done.5 = f32[1,1,2,128,128]{4,3,2,1,0:T(8,128)S(1)} copy-done((f32[1,1,2,128,128]{4,3,2,1,0:T(8,128)S(1)}, f32[1,1,2,128,128]{4,3,2,1,0:T(8,128)}, u32[]{:S(2)}) %copy-start.5) | copy-done | bytes 131096
  7.3 0.0 copy-start.6
  7.3 0.8 %copy-done.6 = f32[1,32,512]{2,1,0:T(8,128)S(1)} copy-done((f32[1,32,512]{2,1,0:T(8,128)S(1)}, f32[1,32,512]{2,1,0:T(8,128)}, u32[]{:S(2)}) %copy-start.6) | copy-done | bytes 65560
  8.2 32.7 %vcycle.1 = (f32[8,128,128]{2,1,0:T(8,128)S(1)}, f32[4,128,128]{2,1,0:T(8,128)S(1)}, f32[2,128,128]{2,1,0:T(8,128)S(1)}, f32[32,128]{1,0:T(8,128)S(1)}) custom-call(s32[8]{0:T(128)S(1)} %bitcast.30, s32[4]{0:T(128)S(1)} %bitcast.31, s32[1,256]{1,0:T(1,128)S(1)} %bitcast.29, s32[1,32]{1,0:T(1,128)S(1)} %bitcast.32, s32[1,128]{1,0:T(1,128)S(1)} %bitcast.33, ...), custom_call_target="tpu_custom_call" | custom-call | tf_op jit(solution)/shard_map/vcycle/pallas_call | solution.py:429
  40.8 0.8 %copy.22 = f32[1,1,8,128,128]{4,3,2,1,0:T(8,128)} copy(f32[1,1,8,128,128]{4,3,2,1,0:T(8,128)S(1)} %bitcast.18) | data formatting | bytes 1048576
  41.6 0.7 %copy.23 = f32[1,1,4,128,128]{4,3,2,1,0:T(8,128)} copy(f32[1,1,4,128,128]{4,3,2,1,0:T(8,128)S(1)} %bitcast.24) | data formatting | bytes 524288
  42.3 0.7 %copy.24 = f32[1,1,2,128,128]{4,3,2,1,0:T(8,128)} copy(f32[1,1,2,128,128]{4,3,2,1,0:T(8,128)S(1)} %bitcast.26) | data formatting | bytes 262144
  43.0 0.6 %copy.25 = f32[1,32,128]{2,1,0:T(8,128)} copy(f32[1,32,128]{2,1,0:T(8,128)S(1)} %bitcast.28) | data formatting | bytes 32768
Async XLA Ops:
  0.6 0.7 %copy-start.13 = (s32[1,1,64]{2,1,0:T(1,128)S(1)}, s32[1,1,64]{2,1,0:T(1,128)}, u32[]{:S(2)}) copy-start(s32[1,1,64]{2,1,0:T(1,128)} %param.26) | copy-start | bytes 772
  0.6 0.7 %copy-start.9 = (s32[1,1,4]{2,1,0:T(1,128)S(1)}, s32[1,1,4]{2,1,0:T(1,128)}, u32[]{:S(2)}) copy-start(s32[1,1,4]{2,1,0:T(1,128)} %param.22) | copy-start | bytes 52
  0.7 0.7 %copy-start.10 = (s32[1,1,32]{2,1,0:T(1,128)S(1)}, s32[1,1,32]{2,1,0:T(1,128)}, u32[]{:S(2)}) copy-start(s32[1,1,32]{2,1,0:T(1,128)} %param.19) | copy-start | bytes 388
  0.7 0.7 %copy-start.11 = (s32[1,1,128]{2,1,0:T(1,128)S(1)}, s32[1,1,128]{2,1,0:T(1,128)}, u32[]{:S(2)}) copy-start(s32[1,1,128]{2,1,0:T(1,128)} %param.23) | copy-start | bytes 1540
  0.7 0.7 %copy-start.12 = (s32[1,1,16]{2,1,0:T(1,128)S(1)}, s32[1,1,16]{2,1,0:T(1,128)}, u32[]{:S(2)}) copy-start(s32[1,1,16]{2,1,0:T(1,128)} %param.24) | copy-start | bytes 196
  0.7 0.7 %copy-start.7 = (s32[1,1,256]{2,1,0:T(1,128)S(1)}, s32[1,1,256]{2,1,0:T(1,128)}, u32[]{:S(2)}) copy-start(s32[1,1,256]{2,1,0:T(1,128)} %param.18) | copy-start | bytes 3076
  0.7 0.7 %copy-start.8 = (s32[1,1,8]{2,1,0:T(1,128)S(1)}, s32[1,1,8]{2,1,0:T(1,128)}, u32[]{:S(2)}) copy-start(s32[1,1,8]{2,1,0:T(1,128)} %param.17) | copy-start | bytes 100
  1.4 1.0 %copy-start = (f32[1,1,8,128,128]{4,3,2,1,0:T(8,128)S(1)}, f32[1,1,8,128,128]{4,3,2,1,0:T(8,128)}, u32[]{:S(2)}) copy-start(f32[1,1,8,128,128]{4,3,2,1,0:T(8,128)} %param.14) | copy-start | bytes 1572868
  2.4 1.0 %copy-start.1 = (f32[1,1,8,128,128]{4,3,2,1,0:T(8,128)S(1)}, f32[1,1,8,128,128]{4,3,2,1,0:T(8,128)}, u32[]{:S(2)}) copy-start(f32[1,1,8,128,128]{4,3,2,1,0:T(8,128)} %param.15) | copy-start | bytes 1572868
  3.5 1.0 %copy-start.2 = (f32[1,1,8,128,128]{4,3,2,1,0:T(8,128)S(1)}, f32[1,1,8,128,128]{4,3,2,1,0:T(8,128)}, u32[]{:S(2)}) copy-start(f32[1,1,8,128,128]{4,3,2,1,0:T(8,128)} %param.16) | copy-start | bytes 1572868
  4.5 0.9 %copy-start.3 = (f32[1,1,4,128,128]{4,3,2,1,0:T(8,128)S(1)}, f32[1,1,4,128,128]{4,3,2,1,0:T(8,128)}, u32[]{:S(2)}) copy-start(f32[1,1,4,128,128]{4,3,2,1,0:T(8,128)} %param.20) | copy-start | bytes 786436
  5.5 0.9 %copy-start.4 = (f32[1,1,4,128,128]{4,3,2,1,0:T(8,128)S(1)}, f32[1,1,4,128,128]{4,3,2,1,0:T(8,128)}, u32[]{:S(2)}) copy-start(f32[1,1,4,128,128]{4,3,2,1,0:T(8,128)} %param.21) | copy-start | bytes 786436
  6.4 0.9 %copy-start.5 = (f32[1,1,2,128,128]{4,3,2,1,0:T(8,128)S(1)}, f32[1,1,2,128,128]{4,3,2,1,0:T(8,128)}, u32[]{:S(2)}) copy-start(f32[1,1,2,128,128]{4,3,2,1,0:T(8,128)} %param.25) | copy-start | bytes 393220
  7.3 0.8 %copy-start.6 = (f32[1,32,512]{2,1,0:T(8,128)S(1)}, f32[1,32,512]{2,1,0:T(8,128)}, u32[]{:S(2)}) copy-start(f32[1,32,512]{2,1,0:T(8,128)} %param.27) | copy-start | bytes 196612

commit v2 on v0

v2 whole, which is shorter than its diff:
```python
import functools
import math
import types

import jax
import jax.numpy as jnp
from jax import lax
from jax.experimental import pallas as pl
from jax.experimental.pallas import tpu as pltpu
from jax.sharding import PartitionSpec as P

MESH = pl.DeviceIdType.MESH
BCELL = 32
CHEB = 6
M1 = 128
S1 = 32
M2 = 64
S2 = 16
UNK = 128
R = 128
NB0 = 8
NB1 = 4
NB2 = 2
COARSE = 512
BARRIER_AFTER = 2

centre = 1.0
spread = 0.5
coarse_weight = 0.5

f32 = jnp.float32
bf16 = jnp.bfloat16


def coefficients():
    ratio_bound = centre / spread
    momentum = 1.0 / ratio_bound
    pairs = []
    for _ in range(CHEB):
        momentum_next = 1.0 / (2.0 * ratio_bound - momentum)
        pairs.append((momentum_next * momentum, 2.0 * momentum_next / spread))
        momentum = momentum_next
    return pairs


STEPS = coefficients()


def dot(a, b):
    return jnp.dot(a, b, preferred_element_type=f32)


def split(value):
    high = value.astype(bf16)
    return high, (value - high.astype(f32)).astype(bf16)


def halves(value):
    return jnp.concatenate(split(value), axis=1)


def product(matrix, vector):
    rows = matrix.shape[0] // 2
    both = dot(matrix[:rows], vector)
    return both[:, :R] + both[:, R:] + dot(matrix[rows:], vector[:, :R])


def stack_parts(target, b, column, value):
    high, low = split(value)
    target[b, :UNK, column : column + UNK] = high
    target[b, UNK:, column : column + UNK] = low


def smoothing(blocks, pattern, source, operator, vectors, answer, residual, update, after, finish):
    for step in range(CHEB + 1):
        now, later = vectors[step % 2], vectors[(step + 1) % 2]
        for b in range(blocks):
            own = now[b]
            if pattern is not None:
                own = jnp.concatenate([own, now[pattern[b]]], axis=0)
            left = (source[b] if step == 0 else residual[b]) - product(operator[b], own)
            if step == CHEB:
                finish(b, left)
                continue
            residual[b] = left
            keep, gain = STEPS[step]
            changed = keep * (source[b] if step == 0 else update[b]) + gain * left
            if step < CHEB - 1:
                update[b] = changed
            answer[b] = (source[b] if step == 0 else answer[b]) + changed
            later[b] = halves(changed)
        after(step)


def selector(rows, targets, weight):
    wanted = lax.broadcasted_iota(jnp.int32, (rows, targets.shape[1]), 0)
    return jnp.where(wanted == targets, jnp.float32(weight), jnp.float32(0.0)).astype(bf16)


def gathered(matrix, vector):
    both = dot(matrix, vector)
    return both[:, :R] + both[:, R:]


def scratch_of(side):
    rows = COARSE // (side * side)

    def vector(blocks):
        return pltpu.VMEM((blocks, UNK, R), f32)

    def operator(blocks):
        return pltpu.VMEM((blocks, 2 * UNK, 2 * UNK), bf16)

    def parts(blocks):
        return pltpu.VMEM((blocks, UNK, 2 * R), bf16)

    def table(width):
        return pltpu.VMEM((1, width), jnp.int32)

    def dma(*shape):
        return pltpu.SemaphoreType.DMA(shape)

    return dict(
        pat_fine=pltpu.SMEM((1, NB0), jnp.int32),
        pat_mid=pltpu.SMEM((1, NB1), jnp.int32),
        map_fine=table(2 * M1),
        map_land_one=table(S1),
        map_mid=table(M1),
        map_land_two=table(S2),
        map_owner=table(M2),
        f_fine=vector(NB0),
        d_fine=vector(NB0),
        c_fine=vector(NB0),
        r_fine=vector(NB0),
        u_fine=vector(NB0),
        a_fine=operator(NB0),
        v_fine0=parts(NB0),
        v_fine1=parts(NB0),
        p_fine=parts(NB0),
        f_mid=vector(NB1),
        d_mid=vector(NB1),
        c_mid=vector(NB1),
        r_mid=vector(NB1),
        u_mid=vector(NB1),
        a_mid=operator(NB1),
        v_mid0=parts(NB1),
        v_mid1=parts(NB1),
        p_mid=parts(NB1),
        f_low=vector(NB2),
        d_low=vector(NB2),
        e_low=vector(NB2),
        x_low=vector(NB2),
        r_low=vector(NB2),
        u_low=vector(NB2),
        a_low=pltpu.VMEM((NB2, 2 * UNK, UNK), bf16),
        pq_low=pltpu.VMEM((NB2, 4 * UNK, UNK), bf16),
        v_low0=parts(NB2),
        v_low1=parts(NB2),
        p_low=parts(NB2),
        inv=pltpu.VMEM((side, side, rows, COARSE), f32),
        send_one=pltpu.VMEM((4, S1, R), f32),
        got_one=pltpu.VMEM((4, S1, R), f32),
        send_two=pltpu.VMEM((4, S2, R), f32),
        got_two=pltpu.VMEM((4, S2, R), f32),
        sums=pltpu.VMEM((COARSE, 2 * R), bf16),
        shares=pltpu.VMEM((side, side, rows, R), f32),
        slots=pltpu.VMEM((side, side, rows, R), f32),
        load_small=dma(7),
        load_d=dma(NB0),
        load_c=dma(NB0),
        load_rest=dma(5),
        one_send=dma(4),
        one_recv=dma(4),
        two_send=dma(4),
        two_recv=dma(4),
        in_send=dma(2, side),
        in_recv=dma(2, side),
        on_send=dma(2, side),
        on_recv=dma(2, side),
        rs_send=dma(side, side),
        rs_recv=dma(side, side),
    )


def kernel(
    n_stream,
    side,
    names,
    pattern_fine,
    pattern_mid,
    restrict_fine,
    landing_one,
    restrict_mid,
    landing_two,
    owner_cells,
    forcing,
    block_fine,
    couple_fine,
    block_mid,
    couple_mid,
    block_low,
    inverse,
    x_fine,
    x_mid,
    y_low,
    fix,
    *scratch,
):
    k = types.SimpleNamespace(**dict(zip(names, scratch)))
    n_cross = side * side
    rows = COARSE // n_cross
    half = rows // 2
    me_s = lax.axis_index("stream")
    me_c = lax.axis_index("cross")
    x = me_c // side
    y = lax.rem(me_c, side)
    ahead = lax.rem(me_s + 1, n_stream)
    behind = lax.rem(me_s + n_stream - 1, n_stream)

    def plus(a, offset):
        return lax.rem(a + offset, side)

    def start(source, target, sem):
        copy = pltpu.make_async_copy(source, target, sem)
        copy.start()
        return copy

    def to_cross(source, target, send, recv, peer_x, peer_y):
        return pltpu.make_async_remote_copy(
            src_ref=source,
            dst_ref=target,
            send_sem=send,
            recv_sem=recv,
            device_id={"cross": peer_x * side + peer_y},
            device_id_type=MESH,
        )

    def to_next(c, source, target, send_sems, recv_sems):
        return pltpu.make_async_remote_copy(
            src_ref=source.at[c],
            dst_ref=target.at[c],
            send_sem=send_sems.at[c],
            recv_sem=recv_sems.at[c],
            device_id={"stream": ahead},
            device_id_type=MESH,
        )

    copy_f = start(forcing, k.f_fine, k.load_rest.at[4])
    copies = []
    for b in range(NB0):
        copies.append(start(block_fine.at[b], k.d_fine.at[b], k.load_d.at[b]))
        copies.append(start(couple_fine.at[b], k.c_fine.at[b], k.load_c.at[b]))
    tables = (
        (pattern_fine, k.pat_fine),
        (pattern_mid, k.pat_mid),
        (restrict_fine, k.map_fine),
        (landing_one, k.map_land_one),
        (restrict_mid, k.map_mid),
        (landing_two, k.map_land_two),
        (owner_cells, k.map_owner),
    )
    small = [start(source, target, k.load_small.at[i]) for i, (source, target) in enumerate(tables)]
    inv = k.inv
    copy_inv = pltpu.make_async_copy(inverse, inv.at[x, y], k.load_rest.at[3])
    copy_inv.start()
    copy_dm = start(block_mid, k.d_mid, k.load_rest.at[0])
    copy_cm = start(couple_mid, k.c_mid, k.load_rest.at[1])
    copy_dl = start(block_low, k.d_low, k.load_rest.at[2])

    barrier = pltpu.get_barrier_semaphore()
    for peer in (ahead, behind):
        pl.semaphore_signal(barrier, inc=1, device_id={"stream": peer}, device_id_type=MESH)
    for offset in range(1, n_cross):
        peer = lax.rem(me_c + offset, n_cross)
        pl.semaphore_signal(barrier, inc=1, device_id={"cross": peer}, device_id_type=MESH)

    copy_f.wait()
    for b in range(NB0):
        k.v_fine0[b] = halves(k.f_fine[b])
    for b in range(NB0):
        copies[2 * b].wait()
        stack_parts(k.a_fine, b, 0, k.d_fine[b])
        copies[2 * b + 1].wait()
        stack_parts(k.a_fine, b, UNK, k.c_fine[b])
    for copy in small:
        copy.wait()
    copy_inv.wait()

    legs = (slice(0, half), slice(half, rows))
    first, second = [], []

    def first_leg():
        for o in range(1, side):
            first.append(to_cross(
                inv.at[x, y, legs[0]], inv.at[x, y, legs[0]],
                k.in_send.at[0, o], k.in_recv.at[0, o], plus(x, o), y,
            ))
            first.append(to_cross(
                inv.at[x, y, legs[1]], inv.at[x, y, legs[1]],
                k.in_send.at[1, o], k.in_recv.at[1, o], x, plus(y, o),
            ))
        for copy in first:
            copy.start()

    def first_leg_arrived():
        for o in range(1, side):
            back_x, back_y = plus(x, side - o), plus(y, side - o)
            to_cross(
                inv.at[back_x, y, legs[0]], inv.at[back_x, y, legs[0]],
                k.in_send.at[0, o], k.in_recv.at[0, o], plus(x, o), y,
            ).wait_recv()
            to_cross(
                inv.at[x, back_y, legs[1]], inv.at[x, back_y, legs[1]],
                k.in_send.at[1, o], k.in_recv.at[1, o], x, plus(y, o),
            ).wait_recv()

    def second_leg():
        for o in range(1, side):
            second.append(to_cross(
                inv.at[:, y, legs[0]], inv.at[:, y, legs[0]],
                k.on_send.at[0, o], k.on_recv.at[0, o], x, plus(y, o),
            ))
            second.append(to_cross(
                inv.at[x, :, legs[1]], inv.at[x, :, legs[1]],
                k.on_send.at[1, o], k.on_recv.at[1, o], plus(x, o), y,
            ))
        for copy in second:
            copy.start()

    def second_leg_arrived():
        for o in range(1, side):
            back_x, back_y = plus(x, side - o), plus(y, side - o)
            to_cross(
                inv.at[:, back_y, legs[0]], inv.at[:, back_y, legs[0]],
                k.on_send.at[0, o], k.on_recv.at[0, o], x, plus(y, o),
            ).wait_recv()
            to_cross(
                inv.at[back_x, :, legs[1]], inv.at[back_x, :, legs[1]],
                k.on_send.at[1, o], k.on_recv.at[1, o], plus(x, o), y,
            ).wait_recv()

    def after_fine(step):
        if step == BARRIER_AFTER:
            pl.semaphore_wait(barrier, n_cross + 1)
            first_leg()

    def finish_fine(b, value):
        k.p_fine[b] = halves(value)

    smoothing(
        NB0, [k.pat_fine[0, b] for b in range(NB0)], k.f_fine, k.a_fine, (k.v_fine0, k.v_fine1),
        x_fine, k.r_fine, k.u_fine, after_fine, finish_fine,
    )

    pick = selector(M1 + S1, k.map_fine[...], coarse_weight)
    to_one = []
    for c in range(4):
        cells = slice(c * BCELL, (c + 1) * BCELL)
        sums = gathered(pick, k.p_fine[:, cells, :].reshape(NB0 * BCELL, 2 * R))
        k.send_one[c] = sums[M1:]
        copy = to_next(c, k.send_one, k.got_one, k.one_send, k.one_recv)
        copy.start()
        to_one.append(copy)
        for b in range(NB1):
            k.f_mid[b, cells, :] = sums[b * BCELL : (b + 1) * BCELL]

    copy_dm.wait()
    copy_cm.wait()
    for b in range(NB1):
        stack_parts(k.a_mid, b, 0, k.d_mid[b])
        stack_parts(k.a_mid, b, UNK, k.c_mid[b])
    first_leg_arrived()
    second_leg()
    copy_dl.wait()
    row = lax.broadcasted_iota(jnp.int32, (UNK, UNK), 0)
    column = lax.broadcasted_iota(jnp.int32, (UNK, UNK), 1)
    for b in range(NB2):
        stack_parts(k.a_low, b, 0, k.d_low[b])
        k.e_low[b] = jnp.where(row == column, jnp.float32(1.0), jnp.float32(0.0))
        k.v_low0[b] = halves(k.e_low[b])

    def finish_low(b, value):
        high, low = split(k.x_low[b])
        k.pq_low[b, 0:UNK] = high
        k.pq_low[b, UNK : 2 * UNK] = low
        high, low = split(value)
        k.pq_low[b, 2 * UNK : 3 * UNK] = high
        k.pq_low[b, 3 * UNK :] = low

    smoothing(
        NB2, None, k.e_low, k.a_low, (k.v_low0, k.v_low1),
        k.x_low, k.r_low, k.u_low, lambda step: None, finish_low,
    )
    land = selector(M1, k.map_land_one[...], 1.0)

    for c in range(4):
        cells = slice(c * BCELL, (c + 1) * BCELL)
        to_one[c].wait_recv()
        landed = gathered(land, halves(k.got_one[c]))
        for b in range(NB1):
            source = k.f_mid[b, cells, :] + landed[b * BCELL : (b + 1) * BCELL]
            k.f_mid[b, cells, :] = source
            k.v_mid0[b, cells, :] = halves(source)

    def finish_mid(b, value):
        k.p_mid[b] = halves(value)

    smoothing(
        NB1, [k.pat_mid[0, b] for b in range(NB1)], k.f_mid, k.a_mid, (k.v_mid0, k.v_mid1),
        x_mid, k.r_mid, k.u_mid, lambda step: None, finish_mid,
    )

    pick = selector(M2 + S2, k.map_mid[...], coarse_weight)
    to_two = []
    for c in range(4):
        cells = slice(c * BCELL, (c + 1) * BCELL)
        sums = gathered(pick, k.p_mid[:, cells, :].reshape(NB1 * BCELL, 2 * R))
        k.send_two[c] = sums[M2:]
        copy = to_next(c, k.send_two, k.got_two, k.two_send, k.two_recv)
        copy.start()
        to_two.append(copy)
        for b in range(NB2):
            k.f_low[b, cells, :] = sums[b * BCELL : (b + 1) * BCELL]

    owners = k.map_owner[...] * 4
    targets = jnp.concatenate(
        [owners[:, b * BCELL : (b + 1) * BCELL] + c for b in range(NB2) for c in range(4)],
        axis=1,
    )
    land = selector(M2, k.map_land_two[...], 1.0)

    for c in range(4):
        cells = slice(c * BCELL, (c + 1) * BCELL)
        to_two[c].wait_recv()
        landed = gathered(land, halves(k.got_two[c]))
        for b in range(NB2):
            k.f_low[b, cells, :] = k.f_low[b, cells, :] + landed[b * BCELL : (b + 1) * BCELL]

    for b in range(NB2):
        vector = halves(k.f_low[b])
        y_low[b] = product(k.pq_low[b, : 2 * UNK], vector)
        k.p_low[b] = halves(product(k.pq_low[b, 2 * UNK :], vector))

    pick = selector(COARSE, targets, coarse_weight)
    k.sums[...] = halves(gathered(pick, k.p_low[...].reshape(NB2 * UNK, 2 * R)))

    second_leg_arrived()
    sums = k.sums[...]
    offsets = [(a, b) for a in range(side) for b in range(side) if a or b]
    offsets.sort(key=lambda o: -(min(o[0], side - o[0]) + min(o[1], side - o[1])))

    def part(px, py):
        return product(jnp.concatenate(split(inv[px, py]), axis=0), sums)

    scattered = []
    for a, b in offsets:
        px, py = plus(x, a), plus(y, b)
        k.shares[a, b] = part(px, py)
        copy = to_cross(
            k.shares.at[a, b], k.slots.at[a, b], k.rs_send.at[a, b], k.rs_recv.at[a, b], px, py
        )
        copy.start()
        scattered.append(copy)
    total = part(x, y)
    for (a, b), copy in reversed(list(zip(offsets, scattered))):
        copy.wait_recv()
        total = total + k.slots[a, b]
    fix[...] = total
    for copy in to_one + to_two + first + second + scattered:
        copy.wait_send()


def write(*refs):
    count = len(refs) // 2
    sems = refs[-1]
    copies = [pltpu.make_async_copy(refs[i], refs[count + i], sems.at[i]) for i in range(count)]
    for copy in copies:
        copy.start()
    for copy in copies:
        copy.wait()


def on_device(n_stream, n_cross, forcing, block_fine, couple_fine, pattern_fine, restrict_fine, landing_one,
              block_mid, couple_mid, pattern_mid, restrict_mid, landing_two, block_low, owner_cells, coarse_inverse):
    side = math.isqrt(n_cross)
    rows = COARSE // n_cross
    anywhere = pl.BlockSpec(memory_space=pl.ANY)
    hbm = pl.BlockSpec(memory_space=pltpu.HBM)
    scratch = scratch_of(side)
    shapes = (
        jax.ShapeDtypeStruct((NB0, UNK, R), f32),
        jax.ShapeDtypeStruct((NB1, UNK, R), f32),
        jax.ShapeDtypeStruct((NB2, UNK, R), f32),
        jax.ShapeDtypeStruct((rows, R), f32),
    )
    made = pl.pallas_call(
        functools.partial(kernel, n_stream, side, tuple(scratch)),
        out_shape=shapes,
        in_specs=[hbm] * 14,
        out_specs=(pl.BlockSpec(memory_space=pltpu.VMEM),) * 4,
        scratch_shapes=list(scratch.values()),
        compiler_params=pltpu.CompilerParams(
            collective_id=0, has_side_effects=True, vmem_limit_bytes=48 << 20
        ),
        name="vcycle",
    )(*(pltpu.with_memory_space_constraint(v, pltpu.HBM) for v in (
        pattern_fine[0],
        pattern_mid[0],
        restrict_fine[0],
        landing_one[0],
        restrict_mid[0],
        landing_two[0],
        owner_cells[0],
        forcing[0, 0],
        block_fine[0, 0],
        couple_fine[0, 0],
        block_mid[0, 0],
        couple_mid[0, 0],
        block_low[0, 0],
        coarse_inverse[0],
        )))
    fine, mid, low, fix = pl.pallas_call(
        write,
        out_shape=shapes,
        in_specs=[pl.BlockSpec(memory_space=pltpu.VMEM)] * 4,
        out_specs=(hbm,) * 4,
        scratch_shapes=[pltpu.SemaphoreType.DMA((4,))],
        name="write",
    )(*(pltpu.with_memory_space_constraint(v, pltpu.VMEM) for v in made))
    return fine[None, None], mid[None, None], low[None, None], fix[None]


def solution(mesh):
    tile = P("stream", "cross", None, None, None)
    table = P("stream", "cross", None)
    return jax.shard_map(
        functools.partial(on_device, mesh.shape["stream"], mesh.shape["cross"]),
        mesh=mesh,
        in_specs=(tile, tile, tile, table, table, table, tile, tile, table, table, table, tile, table, table),
        out_specs=(tile, tile, tile, table),
        check_vma=False,
    )
```

time: 179 us -> 28.5 us (0.16)
  waiting for transfers between devices: 87.9 us -> 0 us
  Pallas kernels: 0 us -> 27.6 us
  local copies, waits for them, and re-layouts: 25 us -> 0 us
  matrix products: 24.6 us -> 0 us
  blocking collectives: 22.1 us -> 0 us
  between operations: 14.7 us -> 0.65 us
  other arithmetic: 3.56 us -> 0 us
    reduce_scatter x1 -> x0, waiting for transfers between devices: 76.8 us -> none  [on_device(): lax.psum_scatter(flat_three, 'cross', scatter_dimension=0, tiled=True)]
    pallas_call x0 -> x2, Pallas kernels: none -> 27.6 us  [the longest x1 26.6 us: on_device(): pl.pallas_call(functools.partial(kernel, n_stream, side, tuple(scratch)),...]
    dot_general x41 -> x0, matrix products: 24.6 us -> none  [the longest x14 12.1 us: apply_blocks(): jnp.einsum('bij,bjr->bir', coupling, jnp.take(vector, pattern, axis=0), p...]
    all_gather x1 -> x0, blocking collectives: 22.1 us -> none  [on_device(): lax.all_gather(owned_share, 'cross', axis=0, tiled=True)]
    gather x14 -> x0, local copies, waits for them, and re-layouts: 15.2 us -> none  [apply_blocks(): jnp.take(vector, pattern, axis=0)]
    ppermute x2 -> x0, waiting for transfers between devices: 11.1 us -> none  [from_behind(): return lax.ppermute(value, axis, pairs)]
    unnamed x56 -> x0, local copies, waits for them, and re-layouts: 8.28 us -> none
    broadcast_in_dim x3 -> x0, other arithmetic: 2.82 us -> none  [the longest x1 1.27 us: on_device(): answer_fine[None, None]]
  transfers between devices with their start and end apart: 3 -> 0, of which waited for: 3 -> 0; matrix products, arithmetic and copies ran while one was open for 0% -> 0% of each run, Pallas kernels for 0% -> 0%
where the time goes in v2:
time: 28.5 us; the launch traced here: 28.2 us
  Pallas kernels  27.6 us (97%)
  between operations  0.65 us (2%)
    pallas_call x1, Pallas kernels, on_device(): pl.pallas_call(functools.partial(kernel, n_stream, side, tuple(scratch)),...  26.6 us
    pallas_call x1, Pallas kernels, on_device(): pl.pallas_call(write, out_shape=shapes, in_specs=[pl.BlockSpec(memory_spa...  0.95 us

profile of v2, /device:TPU:2, one launch (start us, length us, event | category | flops | bytes accessed | tf_op | source)
XLA Modules:
  0.0 28.2 jit_solution(13819109598023047572)
XLA Ops:
  0.6 26.6 %vcycle.1 = (f32[8,128,128]{2,1,0:T(8,128)S(1)}, f32[4,128,128]{2,1,0:T(8,128)S(1)}, f32[2,128,128]{2,1,0:T(8,128)S(1)}, f32[32,128]{1,0:T(8,128)S(1)}) custom-call(s32[1,8]{1,0:T(1,128)} %bitcast.26, s32[1,4]{1,0:T(1,128)} %bitcast.27, s32[1,256]{1,0:T(1,128)} %bitcast.25, s32[1,32]{1,0:T(1,128)} %bitcast.28, s32[1,128]{1,0:T(1,128)} %bitcast.29, ...), custom_call_target="tpu_custom_call" | custom-call | tf_op jit(solution)/shard_map/vcycle/pallas_call | solution.py:496
  27.3 1.0 %write.1 = (f32[8,128,128]{2,1,0:T(8,128)}, f32[4,128,128]{2,1,0:T(8,128)}, f32[2,128,128]{2,1,0:T(8,128)}, f32[32,128]{1,0:T(8,128)}) custom-call(f32[8,128,128]{2,1,0:T(8,128)S(1)} %get-tuple-element.12.refs_0_, f32[4,128,128]{2,1,0:T(8,128)S(1)} %get-tuple-element.13.refs_1_, f32[2,128,128]{2,1,0:T(8,128)S(1)} %get-tuple-element.14.refs_2_, ...), custom_call_target="tpu_custom_call" | custom-call | tf_op jit(solution)/shard_map/write/pallas_call | solution.py:522

commit v3 on v2

--- a/solution.py
+++ b/solution.py
@@ -22,7 +22,7 @@
 NB1 = 4
 NB2 = 2
 COARSE = 512
-BARRIER_AFTER = 2
+BARRIER_AFTER = 0
 
 centre = 1.0
 spread = 0.5
@@ -162,12 +162,13 @@
         got_one=pltpu.VMEM((4, S1, R), f32),
         send_two=pltpu.VMEM((4, S2, R), f32),
         got_two=pltpu.VMEM((4, S2, R), f32),
-        sums=pltpu.VMEM((COARSE, 2 * R), bf16),
-        shares=pltpu.VMEM((side, side, rows, R), f32),
-        slots=pltpu.VMEM((side, side, rows, R), f32),
+        inv_parts=pltpu.VMEM((2 * COARSE, COARSE), bf16),
+        w_parts=pltpu.VMEM((2 * COARSE, NB2 * UNK), bf16),
+        shares=pltpu.VMEM((side * side, rows, R), f32),
+        slots=pltpu.VMEM((side * side, rows, R), f32),
         load_small=dma(7),
-        load_d=dma(NB0),
-        load_c=dma(NB0),
+        load_d=dma(2),
+        load_c=dma(2),
         load_rest=dma(5),
         one_send=dma(4),
         one_recv=dma(4),
@@ -175,10 +176,10 @@
         two_recv=dma(4),
         in_send=dma(2, side),
         in_recv=dma(2, side),
-        on_send=dma(2, side),
-        on_recv=dma(2, side),
-        rs_send=dma(side, side),
-        rs_recv=dma(side, side),
+        on_send=dma(2, side, side),
+        on_recv=dma(2, side, side),
+        rs_send=dma(side * side),
+        rs_recv=dma(side * side),
     )
 
 
@@ -247,13 +248,22 @@
 
     copy_f = start(forcing, k.f_fine, k.load_rest.at[4])
     copies = []
-    for b in range(NB0):
-        copies.append(start(block_fine.at[b], k.d_fine.at[b], k.load_d.at[b]))
-        copies.append(start(couple_fine.at[b], k.c_fine.at[b], k.load_c.at[b]))
+    for i in range(2):
+        part = pl.ds(i * NB0 // 2, NB0 // 2)
+        copies.append(start(block_fine.at[part], k.d_fine.at[part], k.load_d.at[i]))
+        copies.append(start(couple_fine.at[part], k.c_fine.at[part], k.load_c.at[i]))
+
+    barrier = pltpu.get_barrier_semaphore()
+    for peer in (ahead, behind):
+        pl.semaphore_signal(barrier, inc=1, device_id={"stream": peer}, device_id_type=MESH)
+    for o in range(1, side):
+        for peer in (plus(x, o) * side + y, x * side + plus(y, o)):
+            pl.semaphore_signal(barrier, inc=1, device_id={"cross": peer}, device_id_type=MESH)
+
     tables = (
         (pattern_fine, k.pat_fine),
+        (restrict_fine, k.map_fine),
         (pattern_mid, k.pat_mid),
-        (restrict_fine, k.map_fine),
         (landing_one, k.map_land_one),
         (restrict_mid, k.map_mid),
         (landing_two, k.map_land_two),
@@ -261,27 +271,20 @@
     )
     small = [start(source, target, k.load_small.at[i]) for i, (source, target) in enumerate(tables)]
     inv = k.inv
-    copy_inv = pltpu.make_async_copy(inverse, inv.at[x, y], k.load_rest.at[3])
-    copy_inv.start()
+    copy_inv = start(inverse, inv.at[x, y], k.load_rest.at[3])
     copy_dm = start(block_mid, k.d_mid, k.load_rest.at[0])
     copy_cm = start(couple_mid, k.c_mid, k.load_rest.at[1])
     copy_dl = start(block_low, k.d_low, k.load_rest.at[2])
 
-    barrier = pltpu.get_barrier_semaphore()
-    for peer in (ahead, behind):
-        pl.semaphore_signal(barrier, inc=1, device_id={"stream": peer}, device_id_type=MESH)
-    for offset in range(1, n_cross):
-        peer = lax.rem(me_c + offset, n_cross)
-        pl.semaphore_signal(barrier, inc=1, device_id={"cross": peer}, device_id_type=MESH)
-
     copy_f.wait()
     for b in range(NB0):
         k.v_fine0[b] = halves(k.f_fine[b])
-    for b in range(NB0):
-        copies[2 * b].wait()
-        stack_parts(k.a_fine, b, 0, k.d_fine[b])
-        copies[2 * b + 1].wait()
-        stack_parts(k.a_fine, b, UNK, k.c_fine[b])
+    for i in range(2):
+        copies[2 * i].wait()
+        copies[2 * i + 1].wait()
+        for b in range(i * NB0 // 2, (i + 1) * NB0 // 2):
+            stack_parts(k.a_fine, b, 0, k.d_fine[b])
+            stack_parts(k.a_fine, b, UNK, k.c_fine[b])
     for copy in small:
         copy.wait()
     copy_inv.wait()
@@ -290,58 +293,42 @@
     first, second = [], []
 
     def first_leg():
-        for o in range(1, side):
-            first.append(to_cross(
-                inv.at[x, y, legs[0]], inv.at[x, y, legs[0]],
-                k.in_send.at[0, o], k.in_recv.at[0, o], plus(x, o), y,
-            ))
-            first.append(to_cross(
-                inv.at[x, y, legs[1]], inv.at[x, y, legs[1]],
-                k.in_send.at[1, o], k.in_recv.at[1, o], x, plus(y, o),
-            ))
+        for o in (2, 1, 3):
+            first.append(to_cross(inv.at[x, y], inv.at[x, y], k.in_send.at[0, o], k.in_recv.at[0, o], plus(x, o), y))
+            first.append(to_cross(inv.at[x, y], inv.at[x, y], k.in_send.at[1, o], k.in_recv.at[1, o], x, plus(y, o)))
         for copy in first:
             copy.start()
 
-    def first_leg_arrived():
-        for o in range(1, side):
+    def second_leg():
+        for o in (1, 3, 2):
             back_x, back_y = plus(x, side - o), plus(y, side - o)
             to_cross(
-                inv.at[back_x, y, legs[0]], inv.at[back_x, y, legs[0]],
-                k.in_send.at[0, o], k.in_recv.at[0, o], plus(x, o), y,
+                inv.at[back_x, y], inv.at[back_x, y], k.in_send.at[0, o], k.in_recv.at[0, o], plus(x, o), y
             ).wait_recv()
             to_cross(
-                inv.at[x, back_y, legs[1]], inv.at[x, back_y, legs[1]],
-                k.in_send.at[1, o], k.in_recv.at[1, o], x, plus(y, o),
+                inv.at[x, back_y], inv.at[x, back_y], k.in_send.at[1, o], k.in_recv.at[1, o], x, plus(y, o)
             ).wait_recv()
-
-    def second_leg():
-        for o in range(1, side):
-            second.append(to_cross(
-                inv.at[:, y, legs[0]], inv.at[:, y, legs[0]],
-                k.on_send.at[0, o], k.on_recv.at[0, o], x, plus(y, o),
-            ))
-            second.append(to_cross(
-                inv.at[x, :, legs[1]], inv.at[x, :, legs[1]],
-                k.on_send.at[1, o], k.on_recv.at[1, o], plus(x, o), y,
-            ))
-        for copy in second:
-            copy.start()
+            for p in (2, 1, 3):
+                block = inv.at[back_x, y, legs[0]]
+                copy = to_cross(block, block, k.on_send.at[0, o, p], k.on_recv.at[0, o, p], x, plus(y, p))
+                copy.start()
+                second.append(copy)
+                block = inv.at[x, back_y, legs[1]]
+                copy = to_cross(block, block, k.on_send.at[1, o, p], k.on_recv.at[1, o, p], plus(x, p), y)
+                copy.start()
+                second.append(copy)
 
     def second_leg_arrived():
-        for o in range(1, side):
-            back_x, back_y = plus(x, side - o), plus(y, side - o)
-            to_cross(
-                inv.at[:, back_y, legs[0]], inv.at[:, back_y, legs[0]],
-                k.on_send.at[0, o], k.on_recv.at[0, o], x, plus(y, o),
-            ).wait_recv()
-            to_cross(
-                inv.at[back_x, :, legs[1]], inv.at[back_x, :, legs[1]],
-                k.on_send.at[1, o], k.on_recv.at[1, o], plus(x, o), y,
-            ).wait_recv()
+        for o in (1, 3, 2):
+            for p in (2, 1, 3):
+                block = inv.at[plus(x, side - o), plus(y, side - p), legs[0]]
+                to_cross(block, block, k.on_send.at[0, o, p], k.on_recv.at[0, o, p], x, plus(y, p)).wait_recv()
+                block = inv.at[plus(x, side - p), plus(y, side - o), legs[1]]
+                to_cross(block, block, k.on_send.at[1, o, p], k.on_recv.at[1, o, p], plus(x, p), y).wait_recv()
 
     def after_fine(step):
         if step == BARRIER_AFTER:
-            pl.semaphore_wait(barrier, n_cross + 1)
+            pl.semaphore_wait(barrier, 2 * side)
             first_leg()
 
     def finish_fine(b, value):
@@ -352,25 +339,37 @@
         x_fine, k.r_fine, k.u_fine, after_fine, finish_fine,
     )
 
-    pick = selector(M1 + S1, k.map_fine[...], coarse_weight)
-    to_one = []
-    for c in range(4):
-        cells = slice(c * BCELL, (c + 1) * BCELL)
-        sums = gathered(pick, k.p_fine[:, cells, :].reshape(NB0 * BCELL, 2 * R))
-        k.send_one[c] = sums[M1:]
-        copy = to_next(c, k.send_one, k.got_one, k.one_send, k.one_recv)
-        copy.start()
-        to_one.append(copy)
-        for b in range(NB1):
-            k.f_mid[b, cells, :] = sums[b * BCELL : (b + 1) * BCELL]
+    def component(p, c):
+        blocks = p.shape[0]
+        return p[:, c * BCELL : (c + 1) * BCELL, :].reshape(blocks * BCELL, 2 * R)
+
+    def send_straddling(p, table, owned, straddling, target, got, send_sems, recv_sems):
+        pick = selector(straddling, table - owned, coarse_weight)
+        for c in range(4):
+            target[c] = gathered(pick, component(p, c))
+        sent = [to_next(c, target, got, send_sems, recv_sems) for c in range(4)]
+        for copy in sent:
+            copy.start()
+        return sent
+
+    def keep_owned(p, table, owned, target):
+        pick = selector(owned, table, coarse_weight)
+        for c in range(4):
+            sums = gathered(pick, component(p, c))
+            for b in range(owned // BCELL):
+                target[b, c * BCELL : (c + 1) * BCELL, :] = sums[b * BCELL : (b + 1) * BCELL]
+
+    to_one = send_straddling(
+        k.p_fine, k.map_fine[...], M1, S1, k.send_one, k.got_one, k.one_send, k.one_recv
+    )
+    second_leg()
+    keep_owned(k.p_fine, k.map_fine[...], M1, k.f_mid)
 
     copy_dm.wait()
     copy_cm.wait()
     for b in range(NB1):
         stack_parts(k.a_mid, b, 0, k.d_mid[b])
         stack_parts(k.a_mid, b, UNK, k.c_mid[b])
-    first_leg_arrived()
-    second_leg()
     copy_dl.wait()
     row = lax.broadcasted_iota(jnp.int32, (UNK, UNK), 0)
     column = lax.broadcasted_iota(jnp.int32, (UNK, UNK), 1)
@@ -393,9 +392,10 @@
     )
     land = selector(M1, k.map_land_one[...], 1.0)
 
+    for copy in to_one:
+        copy.wait_recv()
     for c in range(4):
         cells = slice(c * BCELL, (c + 1) * BCELL)
-        to_one[c].wait_recv()
         landed = gathered(land, halves(k.got_one[c]))
         for b in range(NB1):
             source = k.f_mid[b, cells, :] + landed[b * BCELL : (b + 1) * BCELL]
@@ -410,61 +410,54 @@
         x_mid, k.r_mid, k.u_mid, lambda step: None, finish_mid,
     )
 
-    pick = selector(M2 + S2, k.map_mid[...], coarse_weight)
-    to_two = []
-    for c in range(4):
-        cells = slice(c * BCELL, (c + 1) * BCELL)
-        sums = gathered(pick, k.p_mid[:, cells, :].reshape(NB1 * BCELL, 2 * R))
-        k.send_two[c] = sums[M2:]
-        copy = to_next(c, k.send_two, k.got_two, k.two_send, k.two_recv)
-        copy.start()
-        to_two.append(copy)
-        for b in range(NB2):
-            k.f_low[b, cells, :] = sums[b * BCELL : (b + 1) * BCELL]
+    to_two = send_straddling(
+        k.p_mid, k.map_mid[...], M2, S2, k.send_two, k.got_two, k.two_send, k.two_recv
+    )
+    keep_owned(k.p_mid, k.map_mid[...], M2, k.f_low)
+    land = selector(M2, k.map_land_two[...], 1.0)
 
     owners = k.map_owner[...] * 4
     targets = jnp.concatenate(
         [owners[:, b * BCELL : (b + 1) * BCELL] + c for b in range(NB2) for c in range(4)],
         axis=1,
     )
-    land = selector(M2, k.map_land_two[...], 1.0)
-
+    pick = selector(COARSE, targets, coarse_weight)
+    offsets = [(a, b) for a in range(side) for b in range(side)]
+    offsets.sort(key=lambda o: -(min(o[0], side - o[0]) + min(o[1], side - o[1])))
+    second_leg_arrived()
+    for i, (a, b) in enumerate(offsets):
+        high, low = split(inv[plus(x, a), plus(y, b)])
+        k.inv_parts[i * rows : (i + 1) * rows] = high
+        k.inv_parts[COARSE + i * rows : COARSE + (i + 1) * rows] = low
+    k.w_parts[...] = dot(k.inv_parts[...], pick).astype(bf16)
+
+    for copy in to_two:
+        copy.wait_recv()
     for c in range(4):
         cells = slice(c * BCELL, (c + 1) * BCELL)
-        to_two[c].wait_recv()
         landed = gathered(land, halves(k.got_two[c]))
         for b in range(NB2):
             k.f_low[b, cells, :] = k.f_low[b, cells, :] + landed[b * BCELL : (b + 1) * BCELL]
 
+    vectors = [halves(k.f_low[b]) for b in range(NB2)]
     for b in range(NB2):
-        vector = halves(k.f_low[b])
-        y_low[b] = product(k.pq_low[b, : 2 * UNK], vector)
-        k.p_low[b] = halves(product(k.pq_low[b, 2 * UNK :], vector))
-
-    pick = selector(COARSE, targets, coarse_weight)
-    k.sums[...] = halves(gathered(pick, k.p_low[...].reshape(NB2 * UNK, 2 * R)))
-
-    second_leg_arrived()
-    sums = k.sums[...]
-    offsets = [(a, b) for a in range(side) for b in range(side) if a or b]
-    offsets.sort(key=lambda o: -(min(o[0], side - o[0]) + min(o[1], side - o[1])))
-
-    def part(px, py):
-        return product(jnp.concatenate(split(inv[px, py]), axis=0), sums)
-
+        k.p_low[b] = halves(product(k.pq_low[b, 2 * UNK :], vectors[b]))
+
+    shares = product(k.w_parts[...], k.p_low[...].reshape(NB2 * UNK, 2 * R))
     scattered = []
-    for a, b in offsets:
-        px, py = plus(x, a), plus(y, b)
-        k.shares[a, b] = part(px, py)
+    for i, (a, b) in enumerate(offsets[:-1]):
+        k.shares[i] = shares[i * rows : (i + 1) * rows]
         copy = to_cross(
-            k.shares.at[a, b], k.slots.at[a, b], k.rs_send.at[a, b], k.rs_recv.at[a, b], px, py
+            k.shares.at[i], k.slots.at[i], k.rs_send.at[i], k.rs_recv.at[i], plus(x, a), plus(y, b)
         )
         copy.start()
         scattered.append(copy)
-    total = part(x, y)
-    for (a, b), copy in reversed(list(zip(offsets, scattered))):
-        copy.wait_recv()
-        total = total + k.slots[a, b]
+    for b in range(NB2):
+        y_low[b] = product(k.pq_low[b, : 2 * UNK], vectors[b])
+    total = shares[COARSE - rows :]
+    for i in reversed(range(n_cross - 1)):
+        scattered[i].wait_recv()
+        total = total + k.slots[i]
     fix[...] = total
     for copy in to_one + to_two + first + second + scattered:
         copy.wait_send()

time: 28.5 us -> 28.5 us (level)
  no operation moved by 1% of the time
where the time goes in v3:
time: 28.5 us; the launch traced here: 28.4 us
  Pallas kernels  27.7 us (97%)
  between operations  0.65 us (2%)
    pallas_call x1, Pallas kernels, on_device(): pl.pallas_call(functools.partial(kernel, n_stream, side, tuple(scratch)),...  26.8 us
    pallas_call x1, Pallas kernels, on_device(): pl.pallas_call(write, out_shape=shapes, in_specs=[pl.BlockSpec(memory_spa...  0.95 us

profile of v3, /device:TPU:2, one launch (start us, length us, event | category | flops | bytes accessed | tf_op | source)
XLA Modules:
  0.0 28.4 jit_solution(3548721374148980326)
XLA Ops:
  0.6 26.8 %vcycle.1 = (f32[8,128,128]{2,1,0:T(8,128)S(1)}, f32[4,128,128]{2,1,0:T(8,128)S(1)}, f32[2,128,128]{2,1,0:T(8,128)S(1)}, f32[32,128]{1,0:T(8,128)S(1)}) custom-call(s32[1,8]{1,0:T(1,128)} %bitcast.26, s32[1,4]{1,0:T(1,128)} %bitcast.27, s32[1,256]{1,0:T(1,128)} %bitcast.25, s32[1,32]{1,0:T(1,128)} %bitcast.28, s32[1,128]{1,0:T(1,128)} %bitcast.29, ...), custom_call_target="tpu_custom_call" | custom-call | tf_op jit(solution)/shard_map/vcycle/pallas_call | solution.py:489
  27.4 1.0 %write.1 = (f32[8,128,128]{2,1,0:T(8,128)}, f32[4,128,128]{2,1,0:T(8,128)}, f32[2,128,128]{2,1,0:T(8,128)}, f32[32,128]{1,0:T(8,128)}) custom-call(f32[8,128,128]{2,1,0:T(8,128)S(1)} %get-tuple-element.12.refs_0_, f32[4,128,128]{2,1,0:T(8,128)S(1)} %get-tuple-element.13.refs_1_, f32[2,128,128]{2,1,0:T(8,128)S(1)} %get-tuple-element.14.refs_2_, ...), custom_call_target="tpu_custom_call" | custom-call | tf_op jit(solution)/shard_map/write/pallas_call | solution.py:515

commit v4 on v3

--- a/solution.py
+++ b/solution.py
@@ -23,6 +23,7 @@
 NB2 = 2
 COARSE = 512
 BARRIER_AFTER = 0
+LOADS = 4
 
 centre = 1.0
 spread = 0.5
@@ -167,15 +168,15 @@
         shares=pltpu.VMEM((side * side, rows, R), f32),
         slots=pltpu.VMEM((side * side, rows, R), f32),
         load_small=dma(7),
-        load_d=dma(2),
-        load_c=dma(2),
+        load_d=dma(LOADS),
+        load_c=dma(LOADS),
         load_rest=dma(5),
         one_send=dma(4),
         one_recv=dma(4),
         two_send=dma(4),
         two_recv=dma(4),
-        in_send=dma(2, side),
-        in_recv=dma(2, side),
+        in_send=dma(2, 2, side),
+        in_recv=dma(2, 2, side),
         on_send=dma(2, side, side),
         on_recv=dma(2, side, side),
         rs_send=dma(side * side),
@@ -248,8 +249,8 @@
 
     copy_f = start(forcing, k.f_fine, k.load_rest.at[4])
     copies = []
-    for i in range(2):
-        part = pl.ds(i * NB0 // 2, NB0 // 2)
+    for i in range(LOADS):
+        part = pl.ds(i * NB0 // LOADS, NB0 // LOADS)
         copies.append(start(block_fine.at[part], k.d_fine.at[part], k.load_d.at[i]))
         copies.append(start(couple_fine.at[part], k.c_fine.at[part], k.load_c.at[i]))
 
@@ -279,10 +280,10 @@
     copy_f.wait()
     for b in range(NB0):
         k.v_fine0[b] = halves(k.f_fine[b])
-    for i in range(2):
+    for i in range(LOADS):
         copies[2 * i].wait()
         copies[2 * i + 1].wait()
-        for b in range(i * NB0 // 2, (i + 1) * NB0 // 2):
+        for b in range(i * NB0 // LOADS, (i + 1) * NB0 // LOADS):
             stack_parts(k.a_fine, b, 0, k.d_fine[b])
             stack_parts(k.a_fine, b, UNK, k.c_fine[b])
     for copy in small:
@@ -292,22 +293,31 @@
     legs = (slice(0, half), slice(half, rows))
     first, second = [], []
 
+    def line_copies(o, kind):
+        along_x = inv.at[x, y, legs[kind]]
+        along_y = inv.at[x, y, legs[1 - kind]]
+        return (
+            to_cross(along_x, along_x, k.in_send.at[kind, 0, o], k.in_recv.at[kind, 0, o], plus(x, o), y),
+            to_cross(along_y, along_y, k.in_send.at[kind, 1, o], k.in_recv.at[kind, 1, o], x, plus(y, o)),
+        )
+
+    def line_arrived(o, kind):
+        along_x = inv.at[plus(x, side - o), y, legs[kind]]
+        along_y = inv.at[x, plus(y, side - o), legs[1 - kind]]
+        to_cross(along_x, along_x, k.in_send.at[kind, 0, o], k.in_recv.at[kind, 0, o], plus(x, o), y).wait_recv()
+        to_cross(along_y, along_y, k.in_send.at[kind, 1, o], k.in_recv.at[kind, 1, o], x, plus(y, o)).wait_recv()
+
     def first_leg():
-        for o in (2, 1, 3):
-            first.append(to_cross(inv.at[x, y], inv.at[x, y], k.in_send.at[0, o], k.in_recv.at[0, o], plus(x, o), y))
-            first.append(to_cross(inv.at[x, y], inv.at[x, y], k.in_send.at[1, o], k.in_recv.at[1, o], x, plus(y, o)))
+        for kind in range(2):
+            for o in (2, 1, 3):
+                first.extend(line_copies(o, kind))
         for copy in first:
             copy.start()
 
     def second_leg():
         for o in (1, 3, 2):
             back_x, back_y = plus(x, side - o), plus(y, side - o)
-            to_cross(
-                inv.at[back_x, y], inv.at[back_x, y], k.in_send.at[0, o], k.in_recv.at[0, o], plus(x, o), y
-            ).wait_recv()
-            to_cross(
-                inv.at[x, back_y], inv.at[x, back_y], k.in_send.at[1, o], k.in_recv.at[1, o], x, plus(y, o)
-            ).wait_recv()
+            line_arrived(o, 0)
             for p in (2, 1, 3):
                 block = inv.at[back_x, y, legs[0]]
                 copy = to_cross(block, block, k.on_send.at[0, o, p], k.on_recv.at[0, o, p], x, plus(y, p))
@@ -362,7 +372,6 @@
     to_one = send_straddling(
         k.p_fine, k.map_fine[...], M1, S1, k.send_one, k.got_one, k.one_send, k.one_recv
     )
-    second_leg()
     keep_owned(k.p_fine, k.map_fine[...], M1, k.f_mid)
 
     copy_dm.wait()
@@ -370,6 +379,7 @@
     for b in range(NB1):
         stack_parts(k.a_mid, b, 0, k.d_mid[b])
         stack_parts(k.a_mid, b, UNK, k.c_mid[b])
+    second_leg()
     copy_dl.wait()
     row = lax.broadcasted_iota(jnp.int32, (UNK, UNK), 0)
     column = lax.broadcasted_iota(jnp.int32, (UNK, UNK), 1)
@@ -423,13 +433,24 @@
     )
     pick = selector(COARSE, targets, coarse_weight)
     offsets = [(a, b) for a in range(side) for b in range(side)]
-    offsets.sort(key=lambda o: -(min(o[0], side - o[0]) + min(o[1], side - o[1])))
+    offsets.sort(key=lambda o: (o[0] * o[1] == 0, -min(o[0], side - o[0]) - min(o[1], side - o[1])))
+    far = (side - 1) * (side - 1)
+
+    def fold(begin, end):
+        count = (end - begin) * rows
+        for i in range(begin, end):
+            high, low = split(inv[plus(x, offsets[i][0]), plus(y, offsets[i][1])])
+            at = (i - begin) * rows
+            k.inv_parts[at : at + rows] = high
+            k.inv_parts[count + at : count + at + rows] = low
+        both = dot(k.inv_parts[: 2 * count], pick).astype(bf16)
+        k.w_parts[2 * begin * rows : 2 * end * rows] = both
+
+    for o in (1, 3, 2):
+        line_arrived(o, 1)
+    fold(far, n_cross)
     second_leg_arrived()
-    for i, (a, b) in enumerate(offsets):
-        high, low = split(inv[plus(x, a), plus(y, b)])
-        k.inv_parts[i * rows : (i + 1) * rows] = high
-        k.inv_parts[COARSE + i * rows : COARSE + (i + 1) * rows] = low
-    k.w_parts[...] = dot(k.inv_parts[...], pick).astype(bf16)
+    fold(0, far)
 
     for copy in to_two:
         copy.wait_recv()
@@ -443,18 +464,25 @@
     for b in range(NB2):
         k.p_low[b] = halves(product(k.pq_low[b, 2 * UNK :], vectors[b]))
 
-    shares = product(k.w_parts[...], k.p_low[...].reshape(NB2 * UNK, 2 * R))
+    vector = k.p_low[...].reshape(NB2 * UNK, 2 * R)
     scattered = []
-    for i, (a, b) in enumerate(offsets[:-1]):
-        k.shares[i] = shares[i * rows : (i + 1) * rows]
-        copy = to_cross(
-            k.shares.at[i], k.slots.at[i], k.rs_send.at[i], k.rs_recv.at[i], plus(x, a), plus(y, b)
-        )
-        copy.start()
-        scattered.append(copy)
+    for begin, end in ((0, far), (far, n_cross)):
+        shares = product(k.w_parts[2 * begin * rows : 2 * end * rows], vector)
+        for i in range(begin, min(end, n_cross - 1)):
+            k.shares[i] = shares[(i - begin) * rows : (i - begin + 1) * rows]
+            copy = to_cross(
+                k.shares.at[i],
+                k.slots.at[i],
+                k.rs_send.at[i],
+                k.rs_recv.at[i],
+                plus(x, offsets[i][0]),
+                plus(y, offsets[i][1]),
+            )
+            copy.start()
+            scattered.append(copy)
+    total = shares[(n_cross - 1 - far) * rows :]
     for b in range(NB2):
         y_low[b] = product(k.pq_low[b, : 2 * UNK], vectors[b])
-    total = shares[COARSE - rows :]
     for i in reversed(range(n_cross - 1)):
         scattered[i].wait_recv()
         total = total + k.slots[i]

time: 28.5 us -> 27.4 us (0.961)
  Pallas kernels: 27.7 us -> 26.3 us
    pallas_call x1, Pallas kernels: 26.8 us -> 25.4 us  [on_device(): pl.pallas_call(functools.partial(kernel, n_stream, side, tuple(scratch)),...]
where the time goes in v4:
time: 27.4 us; the launch traced here: 27 us
  Pallas kernels  26.3 us (96%)
  between operations  0.65 us (2%)
    pallas_call x1, Pallas kernels, on_device(): pl.pallas_call(functools.partial(kernel, n_stream, side, tuple(scratch)),...  25.4 us
    pallas_call x1, Pallas kernels, on_device(): pl.pallas_call(write, out_shape=shapes, in_specs=[pl.BlockSpec(memory_spa...  0.95 us

profile of v4, /device:TPU:2, one launch (start us, length us, event | category | flops | bytes accessed | tf_op | source)
XLA Modules:
  0.0 27.0 jit_solution(15888968620218862503)
XLA Ops:
  0.6 25.4 %vcycle.1 = (f32[8,128,128]{2,1,0:T(8,128)S(1)}, f32[4,128,128]{2,1,0:T(8,128)S(1)}, f32[2,128,128]{2,1,0:T(8,128)S(1)}, f32[32,128]{1,0:T(8,128)S(1)}) custom-call(s32[1,8]{1,0:T(1,128)} %bitcast.26, s32[1,4]{1,0:T(1,128)} %bitcast.27, s32[1,256]{1,0:T(1,128)} %bitcast.25, s32[1,32]{1,0:T(1,128)} %bitcast.28, s32[1,128]{1,0:T(1,128)} %bitcast.29, ...), custom_call_target="tpu_custom_call" | custom-call | tf_op jit(solution)/shard_map/vcycle/pallas_call | solution.py:517
  26.0 1.0 %write.1 = (f32[8,128,128]{2,1,0:T(8,128)}, f32[4,128,128]{2,1,0:T(8,128)}, f32[2,128,128]{2,1,0:T(8,128)}, f32[32,128]{1,0:T(8,128)}) custom-call(f32[8,128,128]{2,1,0:T(8,128)S(1)} %get-tuple-element.12.refs_0_, f32[4,128,128]{2,1,0:T(8,128)S(1)} %get-tuple-element.13.refs_1_, f32[2,128,128]{2,1,0:T(8,128)S(1)} %get-tuple-element.14.refs_2_, ...), custom_call_target="tpu_custom_call" | custom-call | tf_op jit(solution)/shard_map/write/pallas_call | solution.py:543

commit v5 on v4

--- a/solution.py
+++ b/solution.py
@@ -23,7 +23,7 @@
 NB2 = 2
 COARSE = 512
 BARRIER_AFTER = 0
-LOADS = 4
+LOADS = 1
 
 centre = 1.0
 spread = 0.5
@@ -85,11 +85,13 @@
                 continue
             residual[b] = left
             keep, gain = STEPS[step]
-            changed = keep * (source[b] if step == 0 else update[b]) + gain * left
+            last = source[b] if step == 0 else update[b]
+            changed = keep * last + gain * left
+            later[b] = halves(changed)
             if step < CHEB - 1:
                 update[b] = changed
-            answer[b] = (source[b] if step == 0 else answer[b]) + changed
-            later[b] = halves(changed)
+            if step % 2 == 1:
+                answer[b] = (source[b] if step == 1 else answer[b]) + (last + changed)
         after(step)
 
 
@@ -255,8 +257,7 @@
         copies.append(start(couple_fine.at[part], k.c_fine.at[part], k.load_c.at[i]))
 
     barrier = pltpu.get_barrier_semaphore()
-    for peer in (ahead, behind):
-        pl.semaphore_signal(barrier, inc=1, device_id={"stream": peer}, device_id_type=MESH)
+    pl.semaphore_signal(barrier, inc=1, device_id={"stream": behind}, device_id_type=MESH)
     for o in range(1, side):
         for peer in (plus(x, o) * side + y, x * side + plus(y, o)):
             pl.semaphore_signal(barrier, inc=1, device_id={"cross": peer}, device_id_type=MESH)
@@ -338,7 +339,7 @@
 
     def after_fine(step):
         if step == BARRIER_AFTER:
-            pl.semaphore_wait(barrier, 2 * side)
+            pl.semaphore_wait(barrier, 2 * side - 1)
             first_leg()
 
     def finish_fine(b, value):

time: 27.4 us -> 27.4 us (level)
  no operation moved by 1% of the time
where the time goes in v5:
time: 27.4 us; the launch traced here: 26.9 us
  Pallas kernels  26.2 us (96%)
  between operations  0.65 us (2%)
    pallas_call x1, Pallas kernels, on_device(): pl.pallas_call(functools.partial(kernel, n_stream, side, tuple(scratch)),...  25.3 us
    pallas_call x1, Pallas kernels, on_device(): pl.pallas_call(write, out_shape=shapes, in_specs=[pl.BlockSpec(memory_spa...  0.95 us

profile of v5, /device:TPU:2, one launch (start us, length us, event | category | flops | bytes accessed | tf_op | source)
XLA Modules:
  0.0 26.9 jit_solution(8756077916252429939)
XLA Ops:
  0.6 25.3 %vcycle.1 = (f32[8,128,128]{2,1,0:T(8,128)S(1)}, f32[4,128,128]{2,1,0:T(8,128)S(1)}, f32[2,128,128]{2,1,0:T(8,128)S(1)}, f32[32,128]{1,0:T(8,128)S(1)}) custom-call(s32[1,8]{1,0:T(1,128)} %bitcast.26, s32[1,4]{1,0:T(1,128)} %bitcast.27, s32[1,256]{1,0:T(1,128)} %bitcast.25, s32[1,32]{1,0:T(1,128)} %bitcast.28, s32[1,128]{1,0:T(1,128)} %bitcast.29, ...), custom_call_target="tpu_custom_call" | custom-call | tf_op jit(solution)/shard_map/vcycle/pallas_call | solution.py:518
  25.9 1.0 %write.1 = (f32[8,128,128]{2,1,0:T(8,128)}, f32[4,128,128]{2,1,0:T(8,128)}, f32[2,128,128]{2,1,0:T(8,128)}, f32[32,128]{1,0:T(8,128)}) custom-call(f32[8,128,128]{2,1,0:T(8,128)S(1)} %get-tuple-element.12.refs_0_, f32[4,128,128]{2,1,0:T(8,128)S(1)} %get-tuple-element.13.refs_1_, f32[2,128,128]{2,1,0:T(8,128)S(1)} %get-tuple-element.14.refs_2_, ...), custom_call_target="tpu_custom_call" | custom-call | tf_op jit(solution)/shard_map/write/pallas_call | solution.py:544
